TPU v7x, 128 devices: a whole 4x4x4 slice. The times are simulated.
128 devices in a mesh: region: 16 (over z, y), survey: 8 (over x, core).
Axes of the slice: x: 4, y: 4, z: 4, core: 2. Of those that a mesh axis runs over, the one named last changes fastest.
Arguments:
- sensitivity: bfloat16 [512, 512, 4096], P(('region', 'survey')), may hold values from -0.09375 to 0.09375
- observed: float32 [512, 8, 512], P(('region', 'survey')), may hold values from -6 to 6
- data_weight: float32 [512, 512], P(('region', 'survey')), may hold values from 0.5 to 2
- data_counts: int32 [512], P(('region', 'survey')), may hold values from 128 to 512
- tile_bricks: int32 [512, 32], P(('region', 'survey')), may hold values from 0 to 65535, as said below
- start_model: float32 [256, 256, 8, 128], P('region', 'survey'), may hold values from -6 to 6
- active_cells: int32 [256, 256, 128], P('region', 'survey'), may hold values from 0 to 1
- face_links: int32 [256, 256, 128], P('region', 'survey'), may hold values from 0 to 63
- reg_weight: float32 [8], replicated, may hold values from 0.3 to 3
Outputs:
- final_model: float32 [256, 256, 8, 128], P('region', 'survey')
- misfit: float32 [512, 8, 512], P(('region', 'survey'))
Inputs may be any that keep to these rules, and one draw needn't show every extreme that they name: `tile_bricks`: brick b lies on owning device b // 512 (region index times 8 plus survey index), at its slab's layer (b % 512) // 32 and row b % 32. The 128 entries of one device's tiles name bricks of at most 2 per owning device; one owning device, the same for all, is named exactly 2 times by every device's tiles. Entries may repeat.
All inputs are finite; a program needn't handle non-finite values.
Results may differ from a plain program's by a relative error of at most 0.0031.
Values may be sent and summed in bfloat16 or wider, within the bound.
A program may use at most 128 MiB of HBM per device.

v0:
```python
import jax
import jax.numpy as jnp
from jax import lax
from jax.sharding import PartitionSpec as P

ITERS = 2


EPS_SQ = 0.09


def with_halo(shard, sides, width):
    for axis, dim in sides:
        count, length = (lax.axis_size(axis), shard.shape[dim])
        up = [(i, (i + 1) % count) for i in range(count - 1)]
        down = [(j, i) for i, j in up]
        last = lax.slice_in_dim(shard, length - width, length, axis=dim)
        first = lax.slice_in_dim(shard, 0, width, axis=dim)
        before = lax.ppermute(last, axis, up)
        after = lax.ppermute(first, axis, down)
        shard = jnp.concatenate([before, shard, after], axis=dim)
    return shard


def stencil_list(padded):
    centre = padded[1:-1, 1:-1]
    zero_rim = jnp.zeros_like(centre[..., :1])
    neighbours = [
        padded[:-2, 1:-1],
        padded[2:, 1:-1],
        padded[1:-1, :-2],
        padded[1:-1, 2:],
        jnp.concatenate([zero_rim, centre[..., :-1]], axis=3),
        jnp.concatenate([centre[..., 1:], zero_rim], axis=3),
    ]
    return (centre, neighbours)


def irls_weights(centre, neighbours, link_bits, depth_index, active, depth_count):
    smallness = (
        active * (1.0 + 2.0 * depth_index / depth_count) / jnp.sqrt(centre * centre + EPS_SQ)
    )
    offsets = [-1.0, 1.0, 0.0, 0.0, 0.0, 0.0]
    face_weights = []
    for number in range(6):
        depth_level = 1.0 + (2.0 * depth_index + offsets[number]) / depth_count
        difference = centre - neighbours[number]
        face_weights.append(
            link_bits[number] * depth_level / jnp.sqrt(difference * difference + EPS_SQ)
        )
    return (smallness, face_weights)


def reg_gradient(centre, neighbours, smallness, face_weights):
    running = smallness * centre
    for number in range(6):
        running = running + face_weights[number] * (centre - neighbours[number])
    return running


def reg_curvature(centre, neighbours, smallness, face_weights):
    running = smallness * centre * centre
    for number in range(6):
        difference = centre - neighbours[number]
        running = running + 0.5 * face_weights[number] * difference * difference
    return jnp.sum(running, axis=(0, 1, 3))


def widen(field):
    return with_halo(field, (("region", 0), ("survey", 1)), 1)


def fetch_bricks(field_low, asked_ids, slot_of):
    layers, strip_rows, samples, cells_x = field_low.shape
    brick_store = field_low.reshape(layers * strip_rows, samples, cells_x)
    replies = brick_store[asked_ids]
    arrived = lax.all_to_all(replies, ("region", "survey"), split_axis=0, concat_axis=0, tiled=True)
    return arrived.reshape(-1, samples, cells_x)[slot_of]


def return_grads(products, slot_of, asked_ids, layers, strip_rows):
    owners, capacity = asked_ids.shape
    samples, cells_x = (products.shape[1], products.shape[2])
    buffer = jnp.zeros((owners * capacity, samples, cells_x), jnp.float32).at[slot_of].set(products)
    buffer = buffer.reshape(owners, capacity, samples, cells_x)
    arrived = lax.all_to_all(buffer, ("region", "survey"), split_axis=0, concat_axis=0, tiled=True)
    summed = jnp.zeros((layers * strip_rows, samples, cells_x), jnp.float32)
    summed = summed.at[asked_ids.reshape(-1)].add(arrived.reshape(-1, samples, cells_x))
    return summed.reshape(layers, strip_rows, samples, cells_x)


def predict(sensor_view, bricks, tiles, tile_width):
    picked = bricks.reshape(tiles, tile_width, bricks.shape[1], bricks.shape[2])
    return jnp.einsum("tdbx,tbsx->tsd", sensor_view, picked, preferred_element_type=jnp.float32)


def shards(
    sensitivity,
    observed,
    data_weight,
    data_counts,
    tile_bricks,
    start_model,
    active_cells,
    face_links,
    reg_weight,
):
    layers, strip_rows, samples, cells_x = start_model.shape
    tiles, tile_width = tile_bricks.shape
    data_slots = sensitivity.shape[1]
    owners = lax.axis_size("region") * lax.axis_size("survey")
    per_owner = layers * strip_rows
    capacity = max(2, 2 * tiles * tile_width // owners)
    depth_count = layers * lax.axis_size("region")
    sensor_view = sensitivity.reshape(tiles, data_slots, tile_width, cells_x)
    requests = tile_bricks.reshape(-1)
    owner_of = requests // per_owner
    local_of = requests % per_owner
    owner_hits = (owner_of[:, None] == jnp.arange(owners, dtype=jnp.int32)[None, :]).astype(
        jnp.int32
    )
    before = jnp.cumsum(owner_hits, axis=0) - owner_hits
    rank_of = jnp.sum(before * owner_hits, axis=1)
    slot_of = owner_of * capacity + rank_of
    slot_hits = slot_of[:, None] == jnp.arange(owners * capacity, dtype=jnp.int32)[None, :]
    asking = jnp.sum(jnp.where(slot_hits, local_of[:, None], 0), axis=0).reshape(owners, capacity)
    asked_ids = lax.all_to_all(
        asking, ("region", "survey"), split_axis=0, concat_axis=0, tiled=True
    )
    active = active_cells.astype(jnp.float32)[:, :, None, :]
    link_bits = [
        (face_links // 2**number % 2).astype(jnp.float32)[:, :, None, :] for number in range(6)
    ]
    depth_index = (
        (lax.axis_index("region") * layers + jnp.arange(layers, dtype=jnp.int32))
        .astype(jnp.float32)
        .reshape(layers, 1, 1, 1)
    )
    row_mask = (
        jnp.arange(data_slots, dtype=jnp.int32)[None, None, :] < data_counts[:, None, None]
    ).astype(jnp.float32)
    weight_sq = row_mask * (data_weight * data_weight)[:, None, :]
    reg_scale = reg_weight[None, None, :, None]
    model_now = start_model * active
    predicted = predict(
        sensor_view,
        fetch_bricks(model_now.astype(jnp.bfloat16), asked_ids, slot_of),
        tiles,
        tile_width,
    )
    for iteration in range(ITERS):
        weighted = (weight_sq * (predicted - observed)).astype(jnp.bfloat16)
        products = jnp.einsum(
            "tsd,tdbx->tbsx", weighted, sensor_view, preferred_element_type=jnp.float32
        )
        data_grad = return_grads(
            products.reshape(-1, samples, cells_x), slot_of, asked_ids, layers, strip_rows
        )
        model_wide = widen(model_now)
        centre, neighbours = stencil_list(model_wide)
        smallness, face_weights = irls_weights(
            centre, neighbours, link_bits, depth_index, active, depth_count
        )
        gradient = active * data_grad + reg_scale * reg_gradient(
            centre, neighbours, smallness, face_weights
        )
        step_pred = predict(
            sensor_view,
            fetch_bricks(gradient.astype(jnp.bfloat16), asked_ids, slot_of),
            tiles,
            tile_width,
        )
        grad_wide = widen(gradient)
        grad_centre, grad_neighbours = stencil_list(grad_wide)
        reg_curv = reg_curvature(grad_centre, grad_neighbours, smallness, face_weights)
        grad_norm = jnp.sum(gradient * gradient, axis=(0, 1, 3))
        data_curv = jnp.sum(weight_sq * step_pred * step_pred, axis=(0, 2))
        grad_norm, data_curv, reg_curv = lax.psum(
            (grad_norm, data_curv, reg_curv), ("region", "survey")
        )
        step_length = grad_norm / (data_curv + reg_weight * reg_curv)
        model_now = model_now - step_length[None, None, :, None] * gradient
        predicted = predicted - step_length[None, :, None] * step_pred
    misfit = row_mask * data_weight[:, None, :] * (predicted - observed)
    return (model_now, misfit)


def solution(mesh):
    return jax.shard_map(
        shards,
        mesh=mesh,
        in_specs=(
            P(("region", "survey"), None, None),
            P(("region", "survey"), None, None),
            P(("region", "survey"), None),
            P(("region", "survey")),
            P(("region", "survey"), None),
            P("region", "survey", None, None),
            P("region", "survey", None),
            P("region", "survey", None),
            P(),
        ),
        out_specs=(P("region", "survey", None, None), P(("region", "survey"), None, None)),
        check_vma=False,
    )
```

profile of v0, /device:TPU:1, one launch (start us, length us, event | category | flops | bytes accessed | tf_op | source)
XLA Modules:
  0.0 486.8 jit_solution(5865502058159342487)
XLA Ops:
  5.8 5.3 %collective-permute-start = (f32[1,32,8,128]{3,2,1,0:T(8,128)}, f32[1,32,8,128]{3,2,1,0:T(8,128)}, u32[]{:S(2)}, u32[]{:S(2)}) collective-permute-start(f32[1,32,8,128]{3,2,1,0:T(8,128)} %get-tuple-element.34), channel_id=1, source_target_pairs={{0,8},{8,16},{16,24},{24,32},{32,40},{40,48},{48,56},{56,64},{64,7... | collective-permute-start | bytes 393224 | tf_op jit(solution)/shard_map/ppermute | solution.py:19
  12.5 12.5 %all-to-all-start = ((s32[128,1,2]{2,1,0:T(1,128)}), s32[128,1,2]{2,1,0:T(1,128)S(1)}, u32[]{:S(2)}, u32[]{:S(2)}) async-start(s32[128,1,2]{2,1,0:T(1,128)} %bitcast), calls=%async_computation | async-start | bytes 131072 | tf_op jit(solution)/shard_map/all_to_all | solution.py:127
  26.2 8.4 %all-to-all-done = s32[128,1,2]{2,1,0:T(1,128)S(1)} async-done(((s32[128,1,2]{2,1,0:T(1,128)}), s32[128,1,2]{2,1,0:T(1,128)S(1)}, u32[]{:S(2)}, u32[]{:S(2)}) %all-to-all-start) | async-done | bytes 1056 | tf_op jit(solution)/shard_map/all_to_all | solution.py:127
  36.3 4.5 all-to-all-start.1
  41.6 13.0 %all-to-all-done.1 = bf16[128,2,8,128]{3,2,1,0:T(8,128)(2,1)S(1)} async-done(((bf16[128,2,8,128]{3,2,1,0:T(8,128)(2,1)}), bf16[128,2,8,128]{3,2,1,0:T(8,128)(2,1)S(1)}, u32[]{:S(2)}, u32[]{:S(2)}) %all-to-all-start.1) | async-done | bytes 524320 | tf_op jit(solution)/shard_map/all_to_all | solution.py:77
  55.3 8.1 %fusion.45 = f32[4,8,512]{2,1,0:T(8,128)S(1)} fusion(bf16[4,32,8,128]{3,2,1,0:T(8,128)(2,1)S(1)} %bitcast.108, bf16[4,512,4096]{2,1,0:T(8,128)(2,1)} %param.9), kind=kOutput, calls=%fused_computation.125 | convolution fusion | flops 134217728 | bytes 17104896 | tf_op jit(solution)/shard_map/tdbx,tbsx->tsd/dot_general | solution.py:94
  63.4 7.0 %fusion.6 = f32[4,8,32,128]{3,1,2,0:T(8,128)S(1)} fusion(f32[4,8,512]{2,1,0:T(8,128)S(1)} %fusion.45, f32[4,8,512]{2,1,0:T(8,128)S(1)} %copy-done.10, f32[4,512]{1,0:T(4,128)S(1)} %get-tuple-element.45, bf16[4,512,4096]{2,1,0:T(8,128)(2,1)} %param.9), kind=kOutput, calls=%fused_computation.16 | convolution fusion | flops 134266880 | bytes 17440768 | tf_op jit(solution)/shard_map/tsd,tdbx->tbsx/dot_general | solution.py:153
  71.4 12.3 %scatter_fusion = f32[256,8,128]{2,1,0:T(8,128)} fusion(f32[256,8,128]{2,1,0:T(8,128)} %broadcast.388.clone, s32[128]{0:T(128)S(1)} %fusion.90, f32[128,8,128]{2,1,0:T(8,128)S(1)} %bitcast.101), kind=kCustom, calls=%fused_computation.6 | custom fusion | bytes 1573376 | tf_op jit(solution)/shard_map/scatter | solution.py:84
  83.8 5.4 %all-to-all-start.2 = ((f32[128,2,8,128]{3,2,1,0:T(8,128)}), f32[128,2,8,128]{3,2,1,0:T(8,128)}, u32[]{:S(2)}, u32[]{:S(2)}) async-start(f32[128,2,8,128]{3,2,1,0:T(8,128)} %bitcast.15), calls=%async_computation.2 | async-start | bytes 2097152 | tf_op jit(solution)/shard_map/all_to_all | solution.py:86
  99.6 3.2 collective-permute-start.3
  109.7 27.9 %scatter_fusion.1 = f32[512,8,128]{2,1,0:T(8,128)} fusion(f32[512,8,128]{2,1,0:T(8,128)} %broadcast.382.clone, s32[256]{0:T(256)S(1)} %bitcast.110, f32[256,8,128]{2,1,0:T(8,128)} %bitcast.16), kind=kCustom, calls=%fused_computation.7 | custom fusion | flops 262144 | bytes 3146752 | tf_op jit(solution)/shard_map/scatter-add | solution.py:88
  137.6 7.0 %fusion.92 = (bf16[16,32,8,128]{3,2,1,0:T(8,128)(2,1)}, f32[16,32,8,128]{3,2,1,0:T(8,128)S(1)}) fusion(f32[16,32,8,128]{3,2,1,0:T(8,128)S(1)} %get-tuple-element.13, f32[16,32,8,127]{3,2,1,0:T(8,128)} %get-tuple-element.37, f32[16,32,128]{2,1,0:T(8,128)S(1)} %get-tuple-element.41, f32[16,32,8,127]{3,2,1,0:T(8,128)} %get-tuple-element.36, ...), kind=kLoop, calls=%fused_computation.246 | loop fusion | flops 27262976 | bytes 14008352 | tf_op jit(solution)/shard_map/convert_element_type | solution.py:169
  146.0 4.2 collective-permute-start.4
  163.2 11.9 %all-to-all-start.3 = ((bf16[128,2,8,128]{3,2,1,0:T(8,128)(2,1)}), bf16[128,2,8,128]{3,2,1,0:T(8,128)(2,1)}, u32[]{:S(2)}, u32[]{:S(2)}) async-start(bf16[128,2,8,128]{3,2,1,0:T(8,128)(2,1)} %bitcast.103), calls=%async_computation.3 | async-start | bytes 1048576 | tf_op jit(solution)/shard_map/all_to_all | solution.py:77
  175.2 11.9 %fusion.21 = f32[8]{0:T(128)} fusion(f32[16,32,8,128]{3,2,1,0:T(8,128)} %copy-done.2, f32[18,1,8,128]{3,2,1,0:T(8,128)} %collective-permute-done.7, f32[1,32,8,128]{3,2,1,0:T(8,128)} %copy-done.17, f32[1,32,8,128]{3,2,1,0:T(8,128)} %copy-done.18, f32[18,1,8,128]{3,2,1,0:T(8,128)} %collective-permute-done.6, f32[16,32,8,127]{3,2,1,0:T(8,128)} %get-tuple-element.31, ...), kind=kLoop, calls=%fused_computation.45 | loop fusion | flops 39845880 | bytes 15171616 | tf_op jit(solution)/shard_map/reduce_sum | solution.py:66
  191.1 11.6 %fusion.80 = (f32[8]{0:T(128)}, f32[4,8,512]{2,1,0:T(8,128)}) fusion(f32[4,512]{1,0:T(4,128)S(1)} %get-tuple-element.45, bf16[4,32,8,128]{3,2,1,0:T(8,128)(2,1)} %bitcast.107, bf16[4,512,4096]{2,1,0:T(8,128)(2,1)} %param.9), kind=kOutput, calls=%fused_computation.206 | convolution fusion | flops 134266880 | bytes 17113120 | tf_op jit(solution)/shard_map/tdbx,tbsx->tsd/dot_general | solution.py:94
  202.7 65.9 %all-reduce.9 = (f32[8]{0:T(128)}, f32[8]{0:T(128)}, f32[8]{0:T(128)}) all-reduce(f32[8]{0:T(128)} %multiply_reduce_fusion.1, f32[8]{0:T(128)} %get-tuple-element.49, f32[8]{0:T(128)} %fusion.21), channel_id=1, replica_groups=mesh['region'=16,'survey'=8] {'region','survey'}, use_global_device_ids=true, to_apply=%region_6.7 | all-reduce | flops 24 | bytes 192 | tf_op jit(solution)/shard_map/psum | solution.py:178
  269.3 8.9 %fusion.2 = f32[4,8,32,128]{3,1,2,0:T(8,128)} fusion(f32[4,8,512]{2,1,0:T(8,128)S(1)} %copy-done.11, f32[4,512]{1,0:T(4,128)S(1)} %get-tuple-element.45, f32[4,8,512]{2,1,0:T(8,128)S(1)} %copy-done.7, f32[4,8,512]{2,1,0:T(8,128)} %get-tuple-element.50, f32[8]{0:T(128)S(1)} %add_divide_fusion.1, bf16[4,512,4096]{2,1,0:T(8,128)(2,1)} %param.9), kind=kOutput, calls=%fused_computation.12 | convolution fusion | flops 134299648 | bytes 17506336 | tf_op jit(solution)/shard_map/tsd,tdbx->tbsx/dot_general | solution.py:153
  279.3 13.9 %scatter_fusion.2 = f32[256,8,128]{2,1,0:T(8,128)} fusion(f32[256,8,128]{2,1,0:T(8,128)} %broadcast.388, s32[128]{0:T(128)} %copy-done.28, f32[128,8,128]{2,1,0:T(8,128)} %bitcast.100), kind=kCustom, calls=%fused_computation.8 | custom fusion | bytes 1573376 | tf_op jit(solution)/shard_map/scatter | solution.py:84
  293.2 5.6 %all-to-all-start.4 = ((f32[128,2,8,128]{3,2,1,0:T(8,128)}), f32[128,2,8,128]{3,2,1,0:T(8,128)}, u32[]{:S(2)}, u32[]{:S(2)}) async-start(f32[128,2,8,128]{3,2,1,0:T(8,128)} %bitcast.96), calls=%async_computation.4 | async-start | bytes 2097152 | tf_op jit(solution)/shard_map/all_to_all | solution.py:86
  302.0 4.0 collective-permute-start.8
  306.0 8.2 %collective-permute-done.9 = f32[1,32,8,128]{3,2,1,0:T(8,128)S(1)} collective-permute-done((f32[1,32,8,128]{3,2,1,0:T(8,128)S(1)}, f32[1,32,8,128]{3,2,1,0:T(8,128)S(1)}, u32[]{:S(2)}, u32[]{:S(2)}) %collective-permute-start.9) | collective-permute-done | bytes 131104 | tf_op jit(solution)/shard_map/ppermute | solution.py:20
  318.0 3.0 collective-permute-start.10
  325.4 28.2 %scatter_fusion.3 = f32[512,8,128]{2,1,0:T(8,128)} fusion(f32[512,8,128]{2,1,0:T(8,128)} %broadcast.382, s32[256]{0:T(256)S(1)} %bitcast.111, f32[256,8,128]{2,1,0:T(8,128)} %bitcast.29), kind=kCustom, calls=%fused_computation.9 | custom fusion | flops 262144 | bytes 3146752 | tf_op jit(solution)/shard_map/scatter-add | solution.py:88
  353.6 7.1 %fusion.91 = (bf16[16,32,8,128]{3,2,1,0:T(8,128)(2,1)}, f32[16,32,8,128]{3,2,1,0:T(8,128)S(1)}) fusion(f32[16,32,8,128]{3,2,1,0:T(8,128)S(1)} %copy-done.1, f32[16,32,8,127]{3,2,1,0:T(8,128)} %get-tuple-element.29, f32[16,32,128]{2,1,0:T(8,128)S(1)} %get-tuple-element.41, f32[16,32,8,127]{3,2,1,0:T(8,128)} %get-tuple-element.28, ...), kind=kLoop, calls=%fused_computation.245 | loop fusion | flops 27262976 | bytes 14008352 | tf_op jit(solution)/shard_map/convert_element_type | solution.py:169
  362.0 4.5 collective-permute-start.12
  372.4 3.5 collective-permute-start.14
  379.9 14.7 %all-to-all-start.5 = ((bf16[128,2,8,128]{3,2,1,0:T(8,128)(2,1)}), bf16[128,2,8,128]{3,2,1,0:T(8,128)(2,1)}, u32[]{:S(2)}, u32[]{:S(2)}) async-start(bf16[128,2,8,128]{3,2,1,0:T(8,128)(2,1)} %bitcast.102), calls=%async_computation.5 | async-start | bytes 1048576 | tf_op jit(solution)/shard_map/all_to_all | solution.py:77
  394.7 10.8 %fusion.28 = f32[8]{0:T(128)S(1)} fusion(f32[16,32,8,128]{3,2,1,0:T(8,128)} %copy-done.3, f32[18,1,8,128]{3,2,1,0:T(8,128)} %collective-permute-done.15, f32[1,32,8,128]{3,2,1,0:T(8,128)} %copy-done.15, f32[1,32,8,128]{3,2,1,0:T(8,128)} %copy-done.16, f32[18,1,8,128]{3,2,1,0:T(8,128)} %collective-permute-done.14, f32[16,32,8,127]{3,2,1,0:T(8,128)} %get-tuple-element.23, ...), kind=kLoop, calls=%fused_computation.52 | loop fusion | flops 39845880 | bytes 15171616 | tf_op jit(solution)/shard_map/reduce_sum | solution.py:66
  409.9 8.2 %fusion.81 = (f32[8]{0:T(128)S(1)}, f32[4,8,512]{2,1,0:T(8,128)S(1)}) fusion(f32[4,512]{1,0:T(4,128)S(1)} %get-tuple-element.45, bf16[4,32,8,128]{3,2,1,0:T(8,128)(2,1)S(1)} %bitcast.106, bf16[4,512,4096]{2,1,0:T(8,128)(2,1)} %param.9), kind=kOutput, calls=%fused_computation.207 | convolution fusion | flops 134266880 | bytes 17113120 | tf_op jit(solution)/shard_map/tdbx,tbsx->tsd/dot_general | solution.py:94
  418.0 64.6 %all-reduce.8 = (f32[8]{0:T(128)S(1)}, f32[8]{0:T(128)S(1)}, f32[8]{0:T(128)S(1)}) all-reduce(f32[8]{0:T(128)S(1)} %copy-done.32, f32[8]{0:T(128)S(1)} %get-tuple-element.51, f32[8]{0:T(128)S(1)} %fusion.28), channel_id=1, replica_groups=mesh['region'=16,'survey'=8] {'region','survey'}, use_global_device_ids=true, to_apply=%region_14.15 | all-reduce | flops 24 | bytes 192 | tf_op jit(solution)/shard_map/psum | solution.py:178
  482.7 3.3 multiply_subtract_fusion
  (148 shorter events, 77.1 us)
Async XLA Ops:
  3.7 37.1 %copy-start.25 = (f32[4,512]{1,0:T(4,128)S(1)}, f32[4,512]{1,0:T(4,128)}, u32[]{:S(2)}) copy-start(f32[4,512]{1,0:T(4,128)} %param.11) | copy-start | bytes 24580
  3.8 37.1 %copy-start.33 = (s32[4]{0:T(128)S(1)}, s32[4]{0:T(128)}, u32[]{:S(2)}) copy-start(s32[4]{0:T(128)} %param.12) | copy-start | bytes 52
  4.5 93.8 %collective-permute-start.1 = (f32[1,32,8,128]{3,2,1,0:T(8,128)}, f32[1,32,8,128]{3,2,1,0:T(8,128)S(1)}, u32[]{:S(2)}, u32[]{:S(2)}) collective-permute-start(f32[1,32,8,128]{3,2,1,0:T(8,128)} %get-tuple-element.35), channel_id=1, source_target_pairs={{8,0},{16,8},{24,16},{32,24},{40,32},{48,40},{56,48},{64,56},{72,6... | collective-permute-start | bytes 393224 | tf_op jit(solution)/shard_map/ppermute | solution.py:20
  5.8 92.5 %collective-permute-start = (f32[1,32,8,128]{3,2,1,0:T(8,128)}, f32[1,32,8,128]{3,2,1,0:T(8,128)}, u32[]{:S(2)}, u32[]{:S(2)}) collective-permute-start(f32[1,32,8,128]{3,2,1,0:T(8,128)} %get-tuple-element.34), channel_id=1, source_target_pairs={{0,8},{8,16},{16,24},{24,32},{32,40},{40,48},{48,56},{56,64},{64,7... | collective-permute-start | bytes 393224 | tf_op jit(solution)/shard_map/ppermute | solution.py:19
  12.5 22.1 %all-to-all-start = ((s32[128,1,2]{2,1,0:T(1,128)}), s32[128,1,2]{2,1,0:T(1,128)S(1)}, u32[]{:S(2)}, u32[]{:S(2)}) async-start(s32[128,1,2]{2,1,0:T(1,128)} %bitcast), calls=%async_computation | async-start | bytes 131072 | tf_op jit(solution)/shard_map/all_to_all | solution.py:127
  34.6 28.8 %copy-start.14 = (s32[128,1,2]{2,1,0:T(1,128)}, s32[128,1,2]{2,1,0:T(1,128)S(1)}, u32[]{:S(2)}) copy-start(s32[128,1,2]{2,1,0:T(1,128)S(1)} %all-to-all-done) | copy-start | bytes 3076
  36.3 18.2 %all-to-all-start.1 = ((bf16[128,2,8,128]{3,2,1,0:T(8,128)(2,1)}), bf16[128,2,8,128]{3,2,1,0:T(8,128)(2,1)S(1)}, u32[]{:S(2)}, u32[]{:S(2)}) async-start(bf16[128,2,8,128]{3,2,1,0:T(8,128)(2,1)} %bitcast.104), calls=%async_computation.1 | async-start | bytes 1048576 | tf_op jit(solution)/shard_map/all_to_all | solution.py:77
  40.9 30.6 %copy-start.28 = (s32[128]{0:T(128)}, s32[128]{0:T(128)S(1)}, u32[]{:S(2)}) copy-start(s32[128]{0:T(128)S(1)} %fusion.90) | copy-start | bytes 1540
  83.8 24.5 %all-to-all-start.2 = ((f32[128,2,8,128]{3,2,1,0:T(8,128)}), f32[128,2,8,128]{3,2,1,0:T(8,128)}, u32[]{:S(2)}, u32[]{:S(2)}) async-start(f32[128,2,8,128]{3,2,1,0:T(8,128)} %bitcast.15), calls=%async_computation.2 | async-start | bytes 2097152 | tf_op jit(solution)/shard_map/all_to_all | solution.py:86
  99.6 38.0 %collective-permute-start.3 = (f32[18,1,8,128]{3,2,1,0:T(8,128)}, f32[18,1,8,128]{3,2,1,0:T(8,128)}, u32[]{:S(2)}, u32[]{:S(2)}) collective-permute-start(f32[18,1,8,128]{3,2,1,0:T(8,128)} %get-tuple-element.21), channel_id=1, source_target_pairs={{1,0},{2,1},{3,2},{4,3},{5,4},{6,5},{7,6},{9,8},{10,9},{11,10},{12... | collective-permute-start | bytes 221192 | tf_op jit(solution)/shard_map/ppermute | solution.py:20
  102.8 34.8 %collective-permute-start.2 = (f32[18,1,8,128]{3,2,1,0:T(8,128)}, f32[18,1,8,128]{3,2,1,0:T(8,128)}, u32[]{:S(2)}, u32[]{:S(2)}) collective-permute-start(f32[18,1,8,128]{3,2,1,0:T(8,128)} %get-tuple-element.20), channel_id=1, source_target_pairs={{0,1},{1,2},{2,3},{3,4},{4,5},{5,6},{6,7},{8,9},{9,10},{10,11},{11... | collective-permute-start | bytes 221192 | tf_op jit(solution)/shard_map/ppermute | solution.py:19
  144.7 8.3 %collective-permute-start.5 = (f32[1,32,8,128]{3,2,1,0:T(8,128)S(1)}, f32[1,32,8,128]{3,2,1,0:T(8,128)S(1)}, u32[]{:S(2)}, u32[]{:S(2)}) collective-permute-start(f32[1,32,8,128]{3,2,1,0:T(8,128)S(1)} %get-tuple-element.33), channel_id=1, source_target_pairs={{8,0},{16,8},{24,16},{32,24},{40,32},{48,40},{56,48},{64,56},{72,6... | collective-permute-start | bytes 393224 | tf_op jit(solution)/shard_map/ppermute | solution.py:20
  146.0 7.0 %collective-permute-start.4 = (f32[1,32,8,128]{3,2,1,0:T(8,128)S(1)}, f32[1,32,8,128]{3,2,1,0:T(8,128)S(1)}, u32[]{:S(2)}, u32[]{:S(2)}) collective-permute-start(f32[1,32,8,128]{3,2,1,0:T(8,128)S(1)} %get-tuple-element.32), channel_id=1, source_target_pairs={{0,8},{8,16},{16,24},{24,32},{32,40},{40,48},{48,56},{56,64},{64,7... | collective-permute-start | bytes 393224 | tf_op jit(solution)/shard_map/ppermute | solution.py:19
  153.7 21.4 %collective-permute-start.7 = (f32[18,1,8,128]{3,2,1,0:T(8,128)}, f32[18,1,8,128]{3,2,1,0:T(8,128)}, u32[]{:S(2)}, u32[]{:S(2)}) collective-permute-start(f32[18,1,8,128]{3,2,1,0:T(8,128)} %get-tuple-element.19), channel_id=1, source_target_pairs={{1,0},{2,1},{3,2},{4,3},{5,4},{6,5},{7,6},{9,8},{10,9},{11,10},{12... | collective-permute-start | bytes 221192 | tf_op jit(solution)/shard_map/ppermute | solution.py:20
  156.8 18.4 %collective-permute-start.6 = (f32[18,1,8,128]{3,2,1,0:T(8,128)}, f32[18,1,8,128]{3,2,1,0:T(8,128)}, u32[]{:S(2)}, u32[]{:S(2)}) collective-permute-start(f32[18,1,8,128]{3,2,1,0:T(8,128)} %get-tuple-element.18), channel_id=1, source_target_pairs={{0,1},{1,2},{2,3},{3,4},{4,5},{5,6},{6,7},{8,9},{9,10},{10,11},{11... | collective-permute-start | bytes 221192 | tf_op jit(solution)/shard_map/ppermute | solution.py:19
  163.2 25.3 %all-to-all-start.3 = ((bf16[128,2,8,128]{3,2,1,0:T(8,128)(2,1)}), bf16[128,2,8,128]{3,2,1,0:T(8,128)(2,1)}, u32[]{:S(2)}, u32[]{:S(2)}) async-start(bf16[128,2,8,128]{3,2,1,0:T(8,128)(2,1)} %bitcast.103), calls=%async_computation.3 | async-start | bytes 1048576 | tf_op jit(solution)/shard_map/all_to_all | solution.py:77
  191.1 78.2 %copy-start.7 = (f32[4,8,512]{2,1,0:T(8,128)S(1)}, f32[4,8,512]{2,1,0:T(8,128)}, u32[]{:S(2)}) copy-start(f32[4,8,512]{2,1,0:T(8,128)} %copy-done.6) | copy-start | bytes 196612
  191.1 78.2 %copy-start.11 = (f32[4,8,512]{2,1,0:T(8,128)S(1)}, f32[4,8,512]{2,1,0:T(8,128)}, u32[]{:S(2)}) copy-start(f32[4,8,512]{2,1,0:T(8,128)} %param.10) | copy-start | bytes 196612
  279.3 19.5 %copy-start.22 = (f32[8]{0:T(128)S(1)}, f32[8]{0:T(128)}, u32[]{:S(2)}) copy-start(f32[8]{0:T(128)} %copy-done.21) | copy-start | bytes 100
  293.2 30.7 %all-to-all-start.4 = ((f32[128,2,8,128]{3,2,1,0:T(8,128)}), f32[128,2,8,128]{3,2,1,0:T(8,128)}, u32[]{:S(2)}, u32[]{:S(2)}) async-start(f32[128,2,8,128]{3,2,1,0:T(8,128)} %bitcast.96), calls=%async_computation.4 | async-start | bytes 2097152 | tf_op jit(solution)/shard_map/all_to_all | solution.py:86
  300.6 20.4 %copy-start = (f32[16,32,8,128]{3,2,1,0:T(8,128)}, f32[16,32,8,128]{3,2,1,0:T(8,128)S(1)}, u32[]{:S(2)}) copy-start(f32[16,32,8,128]{3,2,1,0:T(8,128)S(1)} %multiply_subtract_fusion.1) | copy-start | bytes 6291460
  300.7 13.5 %collective-permute-start.9 = (f32[1,32,8,128]{3,2,1,0:T(8,128)S(1)}, f32[1,32,8,128]{3,2,1,0:T(8,128)S(1)}, u32[]{:S(2)}, u32[]{:S(2)}) collective-permute-start(f32[1,32,8,128]{3,2,1,0:T(8,128)S(1)} %get-tuple-element.27), channel_id=1, source_target_pairs={{8,0},{16,8},{24,16},{32,24},{40,32},{48,40},{56,48},{64,56},{72,6... | collective-permute-start | bytes 393224 | tf_op jit(solution)/shard_map/ppermute | solution.py:20
  302.0 12.2 %collective-permute-start.8 = (f32[1,32,8,128]{3,2,1,0:T(8,128)S(1)}, f32[1,32,8,128]{3,2,1,0:T(8,128)S(1)}, u32[]{:S(2)}, u32[]{:S(2)}) collective-permute-start(f32[1,32,8,128]{3,2,1,0:T(8,128)S(1)} %get-tuple-element.26), channel_id=1, source_target_pairs={{0,8},{8,16},{16,24},{24,32},{32,40},{40,48},{48,56},{56,64},{64,7... | collective-permute-start | bytes 393224 | tf_op jit(solution)/shard_map/ppermute | solution.py:19
  315.5 38.1 %collective-permute-start.11 = (f32[18,1,8,128]{3,2,1,0:T(8,128)}, f32[18,1,8,128]{3,2,1,0:T(8,128)}, u32[]{:S(2)}, u32[]{:S(2)}) collective-permute-start(f32[18,1,8,128]{3,2,1,0:T(8,128)} %get-tuple-element.17), channel_id=1, source_target_pairs={{1,0},{2,1},{3,2},{4,3},{5,4},{6,5},{7,6},{9,8},{10,9},{11,10},{12... | collective-permute-start | bytes 221192 | tf_op jit(solution)/shard_map/ppermute | solution.py:20
  318.0 35.6 %collective-permute-start.10 = (f32[18,1,8,128]{3,2,1,0:T(8,128)}, f32[18,1,8,128]{3,2,1,0:T(8,128)}, u32[]{:S(2)}, u32[]{:S(2)}) collective-permute-start(f32[18,1,8,128]{3,2,1,0:T(8,128)} %get-tuple-element.16), channel_id=1, source_target_pairs={{0,1},{1,2},{2,3},{3,4},{4,5},{5,6},{6,7},{8,9},{9,10},{10,11},{11... | collective-permute-start | bytes 221192 | tf_op jit(solution)/shard_map/ppermute | solution.py:19
  325.4 28.2 %copy-start.1 = (f32[16,32,8,128]{3,2,1,0:T(8,128)S(1)}, f32[16,32,8,128]{3,2,1,0:T(8,128)}, u32[]{:S(2)}) copy-start(f32[16,32,8,128]{3,2,1,0:T(8,128)} %copy-done) | copy-start | bytes 6291460
  360.7 8.7 %collective-permute-start.13 = (f32[1,32,8,128]{3,2,1,0:T(8,128)S(1)}, f32[1,32,8,128]{3,2,1,0:T(8,128)S(1)}, u32[]{:S(2)}, u32[]{:S(2)}) collective-permute-start(f32[1,32,8,128]{3,2,1,0:T(8,128)S(1)} %get-tuple-element.25), channel_id=1, source_target_pairs={{8,0},{16,8},{24,16},{32,24},{40,32},{48,40},{56,48},{64,56},{72,6... | collective-permute-start | bytes 393224 | tf_op jit(solution)/shard_map/ppermute | solution.py:20
  362.0 7.6 %collective-permute-start.12 = (f32[1,32,8,128]{3,2,1,0:T(8,128)S(1)}, f32[1,32,8,128]{3,2,1,0:T(8,128)S(1)}, u32[]{:S(2)}, u32[]{:S(2)}) collective-permute-start(f32[1,32,8,128]{3,2,1,0:T(8,128)S(1)} %get-tuple-element.24), channel_id=1, source_target_pairs={{0,8},{8,16},{16,24},{24,32},{32,40},{40,48},{48,56},{56,64},{64,7... | collective-permute-start | bytes 393224 | tf_op jit(solution)/shard_map/ppermute | solution.py:19
  370.3 24.3 %collective-permute-start.15 = (f32[18,1,8,128]{3,2,1,0:T(8,128)}, f32[18,1,8,128]{3,2,1,0:T(8,128)}, u32[]{:S(2)}, u32[]{:S(2)}) collective-permute-start(f32[18,1,8,128]{3,2,1,0:T(8,128)} %get-tuple-element.15), channel_id=1, source_target_pairs={{1,0},{2,1},{3,2},{4,3},{5,4},{6,5},{7,6},{9,8},{10,9},{11,10},{12... | collective-permute-start | bytes 221192 | tf_op jit(solution)/shard_map/ppermute | solution.py:20
  372.4 22.2 %collective-permute-start.14 = (f32[18,1,8,128]{3,2,1,0:T(8,128)}, f32[18,1,8,128]{3,2,1,0:T(8,128)}, u32[]{:S(2)}, u32[]{:S(2)}) collective-permute-start(f32[18,1,8,128]{3,2,1,0:T(8,128)} %get-tuple-element.14), channel_id=1, source_target_pairs={{0,1},{1,2},{2,3},{3,4},{4,5},{5,6},{6,7},{8,9},{9,10},{10,11},{11... | collective-permute-start | bytes 221192 | tf_op jit(solution)/shard_map/ppermute | solution.py:19
  379.9 28.1 %all-to-all-start.5 = ((bf16[128,2,8,128]{3,2,1,0:T(8,128)(2,1)}), bf16[128,2,8,128]{3,2,1,0:T(8,128)(2,1)}, u32[]{:S(2)}, u32[]{:S(2)}) async-start(bf16[128,2,8,128]{3,2,1,0:T(8,128)(2,1)} %bitcast.102), calls=%async_computation.5 | async-start | bytes 1048576 | tf_op jit(solution)/shard_map/all_to_all | solution.py:77
  409.9 72.8 %copy-start.24 = (f32[8]{0:T(128)S(1)}, f32[8]{0:T(128)}, u32[]{:S(2)}) copy-start(f32[8]{0:T(128)} %param.17) | copy-start | bytes 100
  (24 other events, 153.6 us)
where the time goes:
time: 491 us; the launch traced here: 487 us
  blocking collectives  131 us (27%)
  other arithmetic  115 us (23%)
  starting transfers between devices  99.9 us (20%)
  local copies, waits for them, and re-layouts  59.5 us (12%)
  matrix products  43.8 us (9%)
  waiting for transfers between devices  37 us (8%)
    psum x2, blocking collectives, shards(): lax.psum((grad_norm, data_curv, reg_curv), ('region', 'survey'))  131 us
    scatter-add x2, other arithmetic, return_grads(): summed.at[asked_ids.reshape(-1)].add(arrived.reshape(-1, samples, cells_x))  56 us
    all_to_all x3, starting transfers between devices, fetch_bricks(): lax.all_to_all(replies, ('region', 'survey'), split_axis=0, concat_axis=0...  31.1 us
    ppermute x8, starting transfers between devices, with_halo(): before = lax.ppermute(last, axis, up)  29.4 us
    dot_general x3, matrix products, predict(): jnp.einsum('tdbx,tbsx->tsd', sensor_view, picked, preferred_element_type=...  27.8 us
    scatter x2, local copies, waits for them, and re-layouts, return_grads(): jnp.zeros((owners * capacity, samples, cells_x), jnp.float32).at[slot_of]  26.2 us
    reduce_sum x2, other arithmetic, reg_curvature(): return jnp.sum(running, axis=(0, 1, 3))  22.7 us
    all_to_all x3, waiting for transfers between devices, fetch_bricks(): lax.all_to_all(replies, ('region', 'survey'), split_axis=0, concat_axis=0...  17 us
  transfers between devices with their start and end apart: 22, of which 7 were waited for; matrix products, arithmetic and copies ran while one was open for 30% of the time, Pallas kernels for 0%

commit v1 on v0

v1 whole, which is shorter than its diff:
```python
import functools

import jax
import jax.numpy as jnp
from jax import lax
from jax.experimental import pallas as pl
from jax.experimental.pallas import tpu as pltpu
from jax.sharding import PartitionSpec as P

MESH = pl.DeviceIdType.MESH
EPS_SQ = 0.09
F32, BF16 = jnp.float32, jnp.bfloat16


def kernel(
    dims,
    slot_of,
    entry_of,
    counts,
    reg_weight,
    ask,
    observed,
    data_weight,
    active,
    links,
    model_hbm,
    sens_hbm,
    model_out,
    grad_out,
    step_out,
    misfit_out,
    sens,
    model,
    grad,
    data_grad,
    sums,
    reg_part,
    w_small,
    w_z,
    w_y,
    w_x,
    low_z,
    asked,
    asked_s,
    picked,
    product,
    predicted,
    residual,
    step_pred,
    sent1,
    sent2,
    sent3,
    sent4,
    sent5,
    came1,
    came2,
    came3,
    came4,
    came5,
    spread,
    one_hot,
    stage_y,
    halo_z,
    halo_y,
    grad_z,
    grad_y,
    sum_mine,
    sum_a,
    sum_b,
    load_sem,
    send_sem,
    recv_sem,
):
    regions, surveys, layers, rows, tiles, width, slots = dims
    owners = regions * surveys
    cells = layers * rows
    depth_count = float(layers * regions)
    region, survey = lax.axis_index("region"), lax.axis_index("survey")
    me = region * surveys + survey

    def device(flat):
        return (flat // surveys, flat % surveys)

    sent = (None, sent1, sent2, sent3, sent4, sent5)
    came = (None, came1, came2, came3, came4, came5)
    barrier = pltpu.get_barrier_semaphore()

    def greet(i, c):
        pl.semaphore_signal(
            barrier, inc=1, device_id=device((me + i) % owners), device_id_type=MESH
        )
        return c

    lax.fori_loop(1, owners, greet, 0)
    load_model = pltpu.make_async_copy(model_hbm, model, load_sem.at[0])
    load_model.start()
    load_sens = pltpu.make_async_copy(sens_hbm, sens, load_sem.at[1])
    load_sens.start()
    pl.semaphore_wait(barrier, owners - 1)

    def remote(src, dst, number, to):
        return pltpu.make_async_remote_copy(
            src_ref=src,
            dst_ref=dst,
            send_sem=send_sem.at[number],
            recv_sem=recv_sem.at[number],
            device_id=to,
            device_id_type=MESH,
        )

    def await_bytes(ref, sem):
        pltpu.make_async_copy(ref, ref, sem).wait()

    def send_ids(i, c):
        to = (me + i) % owners
        remote(ask.at[to], asked.at[me], 0, device(to)).start()
        return c

    lax.fori_loop(1, owners, send_ids, 0)
    asked[me] = ask[me]

    load_model.wait()

    def row_of(ref, b):
        return jnp.broadcast_to(ref[pl.ds(b, 1), :], (8, 128))

    def mask_model(b, c):
        model[b] = model[b] * row_of(active, b).astype(F32)
        return c

    lax.fori_loop(0, cells, mask_model, 0, unroll=8)

    up_z = ((region + 1) % regions, survey)
    down_z = ((region + regions - 1) % regions, survey)
    up_y = (region, (survey + 1) % surveys)
    down_y = (region, (survey + surveys - 1) % surveys)

    def send_halo(field, into_z, into_y, base, stage):
        for z in range(layers):
            stage_y[stage, 0, z] = field[z * rows]
            stage_y[stage, 1, z] = field[z * rows + rows - 1]
        last = (layers - 1) * rows
        remote(field.at[pl.ds(0, rows)], into_z.at[1], base, down_z).start()
        remote(field.at[pl.ds(last, rows)], into_z.at[0], base + 1, up_z).start()
        remote(stage_y.at[stage, 0], into_y.at[1], base + 2, down_y).start()
        remote(stage_y.at[stage, 1], into_y.at[0], base + 3, up_y).start()

    def await_halo(into_z, into_y, base):
        await_bytes(into_z.at[1], recv_sem.at[base])
        await_bytes(into_z.at[0], recv_sem.at[base + 1])
        await_bytes(into_y.at[1], recv_sem.at[base + 2])
        await_bytes(into_y.at[0], recv_sem.at[base + 3])

    def sent_halo(field, base, stage):
        await_bytes(field.at[pl.ds(0, rows)], send_sem.at[base])
        await_bytes(field.at[pl.ds(0, rows)], send_sem.at[base + 1])
        await_bytes(stage_y.at[stage, 0], send_sem.at[base + 2])
        await_bytes(stage_y.at[stage, 1], send_sem.at[base + 3])

    send_halo(model, halo_z, halo_y, 10, 0)

    await_bytes(asked.at[pl.ds(0, owners - 1)], recv_sem.at[0])
    to_scalar = pltpu.make_async_copy(asked, asked_s, load_sem.at[2])
    to_scalar.start()
    to_scalar.wait()

    def exchange(number, first_of, second_of):
        def send(i, c):
            to = (me + i) % owners
            sent[number][2 * to] = first_of(to)
            sent[number][2 * to + 1] = second_of(to)
            two = pl.ds(2 * to, 2)
            remote(
                sent[number].at[two], came[number].at[pl.ds(2 * me, 2)], number, device(to)
            ).start()
            return c

        lax.fori_loop(1, owners, send, 0)
        came[number][2 * me] = first_of(me)
        came[number][2 * me + 1] = second_of(me)

    def fetch(field, number):
        exchange(
            number,
            lambda to: field[asked_s[to, 0, 0]].astype(BF16),
            lambda to: field[asked_s[to, 0, 1]].astype(BF16),
        )

    def give_back(number):
        exchange(
            number,
            lambda to: product[entry_of[2 * to]].astype(BF16),
            lambda to: product[entry_of[2 * to + 1]].astype(BF16),
        )

    def await_round(number):
        await_bytes(came[number].at[pl.ds(0, 2 * owners - 2)], recv_sem.at[number])

    fetch(model, 1)

    ids = jnp.transpose(asked[:, 0, :].astype(F32))
    numbers = lax.broadcasted_iota(jnp.int32, (cells, owners), 0).astype(F32)
    for rank in range(2):
        named = jnp.broadcast_to(ids[2 + rank : 3 + rank, :], (cells, owners))
        one_hot[:, rank * owners : (rank + 1) * owners] = jnp.where(
            numbers == named, 1.0, 0.0
        ).astype(BF16)

    lane = lax.broadcasted_iota(jnp.int32, (8, 128), 1)
    sample = lax.broadcasted_iota(jnp.int32, (8, 128), 0)
    scale = jnp.zeros((8, 128), F32)
    for s in range(8):
        scale = jnp.where(sample == s, reg_weight[s], scale)

    def bit(word, k):
        return ((word // 2**k) % 2).astype(F32)

    def regularize():
        def flux(difference, link):
            weight = link * lax.rsqrt(difference * difference + EPS_SQ)
            return weight, weight * difference

        z_base = (region * layers).astype(F32)
        for y in range(rows):
            link = bit(row_of(links, y), 0) * (1.0 + (2.0 * z_base - 1.0) / depth_count)
            low_z[y] = flux(model[y] - halo_z[0, y], link)[1]

        def one_layer(z, c, last):
            depth = z_base + (z if last else z.astype(F32))
            h_here = 1.0 + 2.0 * depth / depth_count
            h_next = 1.0 + (2.0 * depth + 1.0) / depth_count
            first = model[z * rows]
            _, before = flux(
                first - halo_y[0, z], bit(row_of(links, z * rows), 2) * h_here
            )
            for y in range(rows):
                b = z * rows + y
                here = model[b]
                if last:
                    above = halo_z[1, y]
                else:
                    above = model[b + rows]
                beside = model[b + 1] if y < rows - 1 else halo_y[1, z]
                word = row_of(links, b)
                small = (
                    row_of(active, b).astype(F32) * h_here * lax.rsqrt(here * here + EPS_SQ)
                )
                wz, fz = flux(above - here, bit(word, 1) * h_next)
                wy, fy = flux(beside - here, bit(word, 3) * h_here)
                wx, fx = flux(pltpu.roll(here, 127, 1) - here, bit(word, 5) * h_here)
                total = (
                    small * here
                    + (low_z[y] - fz)
                    + (before - fy)
                    + (pltpu.roll(fx, 1, 1) - fx)
                )
                reg_part[b] = scale * total
                w_small[b] = small
                w_z[b] = wz
                w_y[b] = wy
                w_x[b] = wx
                low_z[y] = fz
                before = fy
            return c

        lax.fori_loop(0, layers - 1, functools.partial(one_layer, last=False), 0)
        one_layer(layers - 1, 0, True)

    def curvature(after):
        def one_layer(z, carry, last):
            norm, curv = carry
            for y in range(rows):
                b = z * rows + y
                here = grad[b]
                if last:
                    above = grad_z[after, y]
                else:
                    above = grad[b + rows]
                beside = grad[b + 1] if y < rows - 1 else grad_y[after, z]
                dz, dy, dx = above - here, beside - here, pltpu.roll(here, 127, 1) - here
                square = here * here
                norm = norm + square
                curv = curv + (
                    (w_small[b] * square + w_z[b] * (dz * dz))
                    + (w_y[b] * (dy * dy) + w_x[b] * (dx * dx))
                )
            return norm, curv

        zero = jnp.zeros((8, 128), F32)
        carry = lax.fori_loop(
            0, layers - 1, functools.partial(one_layer, last=False), (zero, zero)
        )
        norm, curv = one_layer(layers - 1, carry, True)
        return (
            jnp.sum(norm, axis=1, keepdims=True),
            jnp.sum(curv * scale, axis=1, keepdims=True),
        )

    def pick(number):
        def one(e, c):
            t, column = e // width, e % width
            at = pl.ds(pl.multiple_of(column * 128, 128), 128)
            picked[t, :, at] = came[number][slot_of[e]].astype(F32)
            return c

        lax.fori_loop(0, tiles * width, one, 0, unroll=4)

    def forward(t):
        chunk = 1024
        total = jnp.zeros((8, slots), F32)
        for c in range(width * 128 // chunk):
            at = slice(c * chunk, (c + 1) * chunk)
            total = total + lax.dot_general(
                picked[t, :, at].astype(BF16),
                sens[t, :, at],
                (((1,), (1,)), ((), ())),
                preferred_element_type=F32,
            )
        return total

    def backward(t, weighted):
        chunk = 1024
        for c in range(width * 128 // chunk):
            made = lax.dot_general(
                weighted,
                sens[t, :, c * chunk : (c + 1) * chunk],
                (((1,), (0,)), ((), ())),
                preferred_element_type=F32,
            )
            for j in range(chunk // 128):
                entry = t * width + c * (chunk // 128) + j
                product[entry] = made[:, j * 128 : (j + 1) * 128]

    def mask_of(t):
        slot = lax.broadcasted_iota(jnp.int32, (1, slots), 1)
        return jnp.where(slot < counts[t], 1.0, 0.0)

    def weight_of(t):
        weight = data_weight[pl.ds(t, 1), :]
        return mask_of(t) * (weight * weight)

    def scatter(number):
        def widen(d, c):
            spread[pl.ds(pl.multiple_of(d * 8, 8), 8), :] = came[number][d].astype(F32)
            return c

        lax.fori_loop(0, 2 * owners, widen, 0, unroll=8)
        table = one_hot[...]
        for s in range(8):
            first = spread[pl.ds(s, owners, stride=16), :]
            second = spread[pl.ds(8 + s, owners, stride=16), :]
            blocks = jnp.concatenate([first, second], axis=0).astype(BF16)
            sums[pl.ds(s, cells, stride=8), :] = jnp.dot(
                table, blocks, preferred_element_type=F32
            )

    def make_gradient(step):
        def one(b, c):
            total = sums[pl.ds(pl.multiple_of(b * 8, 8), 8), :]
            if step is None:
                data_grad[b] = total
            else:
                total = data_grad[b] - step * total
            grad[b] = row_of(active, b).astype(F32) * total + reg_part[b]
            return c

        lax.fori_loop(0, cells, one, 0, unroll=8)

    def sum_start(mine, number):
        sum_mine[number, 0] = mine
        sum_a[number, survey] = mine

        def send(i, c):
            to = (survey + i) % surveys
            remote(
                sum_mine.at[number, 0], sum_a.at[number, survey], 6 + 2 * number, (region, to)
            ).start()
            return c

        lax.fori_loop(1, surveys, send, 0)

    def sum_end(number):
        await_bytes(sum_a.at[number, pl.ds(0, surveys - 1)], recv_sem.at[6 + 2 * number])
        part = sum_a[number, 0]
        for i in range(1, surveys):
            part = part + sum_a[number, i]
        sum_mine[number, 1] = part
        sum_b[number, region] = part

        def send(i, c):
            to = (region + i) % regions
            remote(
                sum_mine.at[number, 1], sum_b.at[number, region], 7 + 2 * number, (to, survey)
            ).start()
            return c

        lax.fori_loop(1, regions, send, 0)
        await_bytes(sum_b.at[number, pl.ds(0, regions - 1)], recv_sem.at[7 + 2 * number])
        whole = sum_b[number, 0]
        for i in range(1, regions):
            whole = whole + sum_b[number, i]
        norm = jnp.sum(jnp.where(lane == 0, whole, 0.0), axis=1, keepdims=True)
        curv = jnp.sum(jnp.where(lane == 1, whole, 0.0), axis=1, keepdims=True)
        return norm / curv

    def my_sums(norm, reg_curv, data_curv):
        return jnp.where(lane == 0, norm, jnp.where(lane == 1, reg_curv + data_curv, 0.0))

    await_halo(halo_z, halo_y, 10)
    regularize()
    load_sens.wait()

    await_round(1)
    pick(1)

    def first_pass(t, c):
        gap = forward(t) - observed[t]
        residual[t] = gap
        backward(t, (weight_of(t) * gap).astype(BF16))
        return c

    lax.fori_loop(0, tiles, first_pass, 0)
    give_back(2)
    await_round(2)
    scatter(2)
    make_gradient(None)
    fetch(grad, 3)
    send_halo(grad, grad_z, grad_y, 14, 1)
    await_halo(grad_z, grad_y, 14)
    norm, reg_curv = curvature(1)

    await_round(3)
    pick(3)

    def second_pass(t, total):
        made = forward(t)
        step_pred[t] = made
        scaled = weight_of(t) * made
        backward(t, scaled.astype(BF16))
        return total + jnp.sum(scaled * made, axis=1, keepdims=True)

    data_curv = lax.fori_loop(0, tiles, second_pass, jnp.zeros((8, 1), F32))
    sum_start(my_sums(norm, reg_curv, data_curv), 0)
    give_back(4)
    step = sum_end(0)
    sent_halo(model, 10, 0)
    sent_halo(grad, 14, 1)
    step_row = jnp.broadcast_to(step, (8, 128))

    def move(b, c):
        model[b] = model[b] - step_row * grad[b]
        return c

    lax.fori_loop(0, cells, move, 0, unroll=8)
    for side in range(2):
        for y in range(rows):
            halo_z[side, y] = halo_z[side, y] - step_row * grad_z[side, y]
        for z in range(layers):
            halo_y[side, z] = halo_y[side, z] - step_row * grad_y[side, z]
    save_model = pltpu.make_async_copy(model, model_out, load_sem.at[3])
    save_model.start()
    regularize()

    def move_gap(t, c):
        residual[t] = residual[t] - step * step_pred[t]
        return c

    lax.fori_loop(0, tiles, move_gap, 0)

    await_round(4)
    scatter(4)
    make_gradient(step_row)
    fetch(grad, 5)
    save_grad = pltpu.make_async_copy(grad, grad_out, load_sem.at[4])
    save_grad.start()
    for z in range(layers):
        stage_y[2, 0, z] = grad[z * rows]
    remote(grad.at[pl.ds(0, rows)], grad_z.at[2], 18, down_z).start()
    remote(stage_y.at[2, 0], grad_y.at[2], 19, down_y).start()
    await_bytes(grad_z.at[2], recv_sem.at[18])
    await_bytes(grad_y.at[2], recv_sem.at[19])
    norm, reg_curv = curvature(2)

    await_round(5)
    pick(5)

    def third_pass(t, total):
        made = forward(t)
        step_pred[t] = made
        return total + jnp.sum(weight_of(t) * made * made, axis=1, keepdims=True)

    data_curv = lax.fori_loop(0, tiles, third_pass, jnp.zeros((8, 1), F32))
    sum_start(my_sums(norm, reg_curv, data_curv), 1)
    step = sum_end(1)
    step_out[...] = jnp.broadcast_to(step, (8, 128))

    def finish(t, c):
        weight = mask_of(t) * data_weight[pl.ds(t, 1), :]
        misfit_out[t] = weight * (residual[t] - step * step_pred[t])
        return c

    lax.fori_loop(0, tiles, finish, 0)

    await_bytes(ask.at[pl.ds(0, owners - 1)], send_sem.at[0])
    for number in range(1, 6):
        await_bytes(sent[number].at[pl.ds(0, 2 * owners - 2)], send_sem.at[number])
    for number in range(2):
        await_bytes(sum_a.at[number, pl.ds(0, surveys - 1)], send_sem.at[6 + 2 * number])
        await_bytes(sum_b.at[number, pl.ds(0, regions - 1)], send_sem.at[7 + 2 * number])
    await_bytes(grad.at[pl.ds(0, rows)], send_sem.at[18])
    await_bytes(stage_y.at[2, 0], send_sem.at[19])
    save_model.wait()
    save_grad.wait()


def shards(
    regions,
    surveys,
    sensitivity,
    observed,
    data_weight,
    data_counts,
    tile_bricks,
    start_model,
    active_cells,
    face_links,
    reg_weight,
):
    layers, rows, samples, across = start_model.shape
    tiles, width = tile_bricks.shape
    slots = sensitivity.shape[1]
    owners, cells = regions * surveys, layers * rows
    entries = tiles * width

    wanted = tile_bricks.reshape(entries)
    owner_of, local_of = wanted // cells, wanted % cells
    number = jnp.arange(entries, dtype=jnp.int32)
    earlier = (owner_of[:, None] == owner_of[None, :]) & (number[None, :] < number[:, None])
    rank_of = jnp.sum(earlier.astype(jnp.int32), axis=1)
    slot_of = 2 * owner_of + rank_of
    hits = jnp.arange(2 * owners, dtype=jnp.int32)[:, None] == slot_of[None, :]
    ask = jnp.sum(jnp.where(hits, local_of[None, :] + 1, 0), axis=1) - 1
    entry_of = jnp.sum(jnp.where(hits, number[None, :], 0), axis=1)
    ask = ask.reshape(owners, 1, 2)
    ask = jnp.concatenate([jnp.maximum(ask, 0), ask], axis=2)
    ask = jnp.pad(ask, ((0, 0), (0, 0), (0, 124)))

    field = jax.ShapeDtypeStruct((cells, samples, across), F32)
    field_scratch = pltpu.VMEM(field.shape, F32)
    blocks = pltpu.VMEM((2 * owners, samples, across), BF16)
    data_scratch = pltpu.VMEM((tiles, samples, slots), F32)
    vmem = pl.BlockSpec(memory_space=pltpu.VMEM)
    smem = pl.BlockSpec(memory_space=pltpu.SMEM)
    anywhere = pl.BlockSpec(memory_space=pl.ANY)
    moved, gradient, step, misfit = pl.pallas_call(
        functools.partial(kernel, (regions, surveys, layers, rows, tiles, width, slots)),
        name="inversion",
        out_shape=(
            field,
            field,
            jax.ShapeDtypeStruct((samples, across), F32),
            jax.ShapeDtypeStruct((tiles, samples, slots), F32),
        ),
        in_specs=[smem] * 4 + [vmem] * 5 + [anywhere] * 2,
        out_specs=(anywhere, anywhere, vmem, vmem),
        scratch_shapes=[
            pltpu.VMEM(sensitivity.shape, BF16),
            field_scratch,
            field_scratch,
            field_scratch,
            pltpu.VMEM((cells * samples, across), F32),
            *[field_scratch] * 5,
            pltpu.VMEM((rows, 8, 128), F32),
            pltpu.VMEM((owners, 1, 128), jnp.int32),
            pltpu.SMEM((owners, 1, 128), jnp.int32),
            pltpu.VMEM((tiles, samples, width * 128), F32),
            pltpu.VMEM((entries, samples, across), F32),
            data_scratch,
            data_scratch,
            data_scratch,
            *[blocks] * 10,
            pltpu.VMEM((owners * 16, 128), F32),
            pltpu.VMEM((cells, 2 * owners), BF16),
            pltpu.VMEM((3, 2, layers, 8, 128), F32),
            pltpu.VMEM((2, rows, 8, 128), F32),
            pltpu.VMEM((2, layers, 8, 128), F32),
            pltpu.VMEM((3, rows, 8, 128), F32),
            pltpu.VMEM((3, layers, 8, 128), F32),
            pltpu.VMEM((2, 2, 8, 128), F32),
            pltpu.VMEM((2, surveys, 8, 128), F32),
            pltpu.VMEM((2, regions, 8, 128), F32),
            pltpu.SemaphoreType.DMA((5,)),
            pltpu.SemaphoreType.DMA((20,)),
            pltpu.SemaphoreType.DMA((20,)),
        ],
        compiler_params=pltpu.CompilerParams(
            collective_id=0, has_side_effects=True, vmem_limit_bytes=60 << 20
        ),
    )(
        slot_of,
        entry_of,
        data_counts,
        reg_weight,
        ask,
        observed,
        data_weight,
        active_cells.reshape(cells, across),
        face_links.reshape(cells, across),
        start_model.reshape(cells, samples, across),
        sensitivity,
    )
    final = moved.reshape(start_model.shape) - step * gradient.reshape(start_model.shape)
    return final, misfit


def solution(mesh):
    return jax.shard_map(
        functools.partial(shards, mesh.shape["region"], mesh.shape["survey"]),
        mesh=mesh,
        in_specs=(
            P(("region", "survey"), None, None),
            P(("region", "survey"), None, None),
            P(("region", "survey"), None),
            P(("region", "survey")),
            P(("region", "survey"), None),
            P("region", "survey", None, None),
            P("region", "survey", None),
            P("region", "survey", None),
            P(),
        ),
        out_specs=(P("region", "survey", None, None), P(("region", "survey"), None, None)),
        check_vma=False,
    )
```

time: 491 us -> 132 us (0.27)
  blocking collectives: 131 us -> 0 us
  Pallas kernels: 0 us -> 124 us
  other arithmetic: 115 us -> 5.06 us
  starting transfers between devices: 99.9 us -> 0 us
  local copies, waits for them, and re-layouts: 59.5 us -> 2.22 us
  matrix products: 43.8 us -> 0 us
  waiting for transfers between devices: 37 us -> 0 us
    psum x2 -> x0, blocking collectives: 131 us -> none  [shards(): lax.psum((grad_norm, data_curv, reg_curv), ('region', 'survey'))]
    pallas_call x0 -> x1, Pallas kernels: none -> 124 us  [shards(): pl.pallas_call(functools.partial(kernel, (regions, surveys, layers, rows,...]
    scatter-add x2 -> x0, other arithmetic: 56 us -> none  [return_grads(): summed.at[asked_ids.reshape(-1)].add(arrived.reshape(-1, samples, cells_x))]
    all_to_all x6 -> x0, starting transfers between devices: 54.6 us -> none  [the longest x3 31.1 us: fetch_bricks(): lax.all_to_all(replies, ('region', 'survey'), split_axis=0, concat_axis=0...]
    ppermute x16 -> x0, starting transfers between devices: 45.4 us -> none  [the longest x8 29.4 us: with_halo(): before = lax.ppermute(last, axis, up)]
    dot_general x5 -> x0, matrix products: 43.8 us -> none  [the longest x3 27.8 us: predict(): jnp.einsum('tdbx,tbsx->tsd', sensor_view, picked, preferred_element_type=...]
    all_to_all x6 -> x0, waiting for transfers between devices: 28.4 us -> none  [the longest x3 17 us: fetch_bricks(): lax.all_to_all(replies, ('region', 'survey'), split_axis=0, concat_axis=0...]
    scatter x2 -> x0, local copies, waits for them, and re-layouts: 26.2 us -> none  [return_grads(): jnp.zeros((owners * capacity, samples, cells_x), jnp.float32).at[slot_of]]
  transfers between devices with their start and end apart: 22 -> 0, of which waited for: 7 -> 0; matrix products, arithmetic and copies ran while one was open for 30% -> 0% of each run, Pallas kernels for 0% -> 0%
where the time goes in v1:
time: 132 us
  Pallas kernels  124 us (94%)
  other arithmetic  5.06 us (4%)
  local copies, waits for them, and re-layouts  2.22 us (2%)
    pallas_call x1, Pallas kernels, shards(): pl.pallas_call(functools.partial(kernel, (regions, surveys, layers, rows,...  124 us
    sub x1, other arithmetic, shards(): moved.reshape(start_model.shape)  3.86 us

profile of v1, /device:TPU:1, one launch (start us, length us, event | category | flops | bytes accessed | tf_op | source)
XLA Modules:
  0.0 132.2 jit_solution(2892207408361423091)
XLA Ops:
  0.6 0.8 reshape.138
  1.4 0.2 convert_reduce_fusion
  1.6 0.0 copy-start.1
  1.6 0.7 select_reduce_fusion
  2.3 0.1 sub.17
  2.5 0.1 broadcast_maximum_fusion
  2.5 0.2 pad_add_fusion
  2.8 0.7 pad.4.ask
  3.4 0.0 copy-done.1
  3.4 124.2 %inversion.1 = (f32[512,8,128]{2,1,0:T(8,128)}, f32[512,8,128]{2,1,0:T(8,128)}, f32[8,128]{1,0:T(8,128)}, f32[4,8,512]{2,1,0:T(8,128)}) custom-call(s32[128]{0:T(128)} %copy-done.1, s32[256]{0:T(256)} %get-tuple-element.11.entry_of, s32[4]{0:T(128)} %counts.1, f32[8]{0:T(128)} %reg_weight.1, s32[128,1,128]{2,1,0:T(1,128)} %pad.4.ask, f32[4,8,512]{2,1,0:T(8,128)} %observed.1, ...), custom_call_target="tpu_custom_call" | custom-call | tf_op jit(solution)/shard_map/inversion/pallas_call | solution.py:555
  127.7 0.0 copy-start
  127.7 3.9 %multiply_subtract_fusion = f32[16,32,8,128]{3,2,1,0:T(8,128)} fusion(f32[16,32,8,128]{3,2,1,0:T(8,128)} %bitcast.6, f32[16,32,8,128]{3,2,1,0:T(8,128)} %bitcast.7, f32[8,128]{1,0:T(8,128)} %get-tuple-element.7), kind=kLoop, calls=%fused_computation | loop fusion | flops 1048576 | bytes 6295552 | tf_op jit(solution)/shard_map/sub | solution.py:612
  131.5 0.0 copy-done
  131.5 0.6 copy.26
  (3 shorter events, 0.0 us)
Async XLA Ops:
  1.6 1.9 %copy-start.1 = (s32[128]{0:T(128)}, s32[128]{0:T(128)S(1)}, u32[]{:S(2)}) copy-start(s32[128]{0:T(128)S(1)} %multiply_add_fusion.slot_of) | copy-start | bytes 1540
  127.7 3.9 %copy-start = (f32[4,8,512]{2,1,0:T(8,128)S(1)}, f32[4,8,512]{2,1,0:T(8,128)}, u32[]{:S(2)}) copy-start(f32[4,8,512]{2,1,0:T(8,128)} %get-tuple-element.17) | copy-start | bytes 196612

commit v2 on v1

--- a/solution.py
+++ b/solution.py
@@ -14,15 +14,13 @@
 
 def kernel(
     dims,
-    slot_of,
-    entry_of,
     counts,
     reg_weight,
-    ask,
-    observed,
-    data_weight,
-    active,
-    links,
+    bricks,
+    observed_hbm,
+    data_weight_hbm,
+    active_hbm,
+    links_hbm,
     model_hbm,
     sens_hbm,
     model_out,
@@ -39,12 +37,27 @@
     w_z,
     w_y,
     w_x,
+    observed,
+    data_weight,
+    active,
+    links,
+    is_active,
+    face_small,
+    face_z,
+    face_y,
+    face_x,
+    first_z,
+    first_y,
     low_z,
+    ask,
     asked,
     asked_s,
+    slot_row,
+    entry_rows,
+    slot_of,
+    entry_of,
     picked,
     product,
-    predicted,
     residual,
     step_pred,
     sent1,
@@ -60,6 +73,8 @@
     spread,
     one_hot,
     stage_y,
+    stage_grad_z,
+    stage_grad_y,
     halo_z,
     halo_y,
     grad_z,
@@ -92,10 +107,48 @@
         return c
 
     lax.fori_loop(1, owners, greet, 0)
-    load_model = pltpu.make_async_copy(model_hbm, model, load_sem.at[0])
-    load_model.start()
-    load_sens = pltpu.make_async_copy(sens_hbm, sens, load_sem.at[1])
-    load_sens.start()
+    def load(src, dst, number):
+        copy = pltpu.make_async_copy(src, dst, load_sem.at[number])
+        copy.start()
+        return copy
+
+    load_links = load(links_hbm, links, 0)
+    load_active = load(active_hbm, active, 1)
+    load_model = load(model_hbm, model, 2)
+    load_observed = load(observed_hbm, observed, 3)
+    load_weight = load(data_weight_hbm, data_weight, 4)
+    load_sens = load(sens_hbm, sens, 5)
+
+    entries = tiles * width
+    wanted = jnp.concatenate([bricks[t : t + 1, :] for t in range(tiles)], axis=1)
+    wanted = jnp.broadcast_to(wanted, (entries, entries))
+    upright = lax.broadcasted_iota(jnp.int32, (entries, entries), 0)
+    across = lax.broadcasted_iota(jnp.int32, (entries, entries), 1)
+    owner = lax.shift_right_logical(wanted, cells.bit_length() - 1)
+    local = jnp.bitwise_and(wanted, cells - 1)
+
+    def count(hit, value, axis):
+        return jnp.sum(jnp.where(hit, value, 0), axis=axis, keepdims=True)
+
+    def square(line):
+        return jnp.broadcast_to(line, (entries, entries))
+
+    owner_col = square(count(upright == across, owner, 1))
+    same = owner == owner_col
+    rank_col = square(count(same & (across < upright), 1, 1))
+    rank_row = square(count(same & (upright < across), 1, 0))
+    slot_row[...] = jnp.minimum(2 * owner + rank_row, 2 * owners - 1)[0:1, :]
+    mine = owner == upright
+    theirs = owner_col == across
+    table = jnp.zeros((owners, 128), jnp.int32)
+    for rank in range(2):
+        number = count(mine & (rank_row == rank), local + 1, 1) - 1
+        table = jnp.where(across == rank, jnp.maximum(number, 0), table)
+        table = jnp.where(across == 2 + rank, number, table)
+        entry_rows[rank : rank + 1, :] = count(theirs & (rank_col == rank), upright, 0)
+    ask[...] = table.reshape(owners, 1, 128)
+    load_slots = load(slot_row, slot_of, 6)
+    load_entries = load(entry_rows, entry_of, 7)
     pl.semaphore_wait(barrier, owners - 1)
 
     def remote(src, dst, number, to):
@@ -119,13 +172,46 @@
     lax.fori_loop(1, owners, send_ids, 0)
     asked[me] = ask[me]
 
-    load_model.wait()
-
     def row_of(ref, b):
         return jnp.broadcast_to(ref[pl.ds(b, 1), :], (8, 128))
 
+    z_base = (region * layers).astype(F32)
+
+    load_links.wait()
+    load_active.wait()
+
+    def prepare(z, c):
+        depth = z_base + z.astype(F32)
+        h_here = 1.0 + 2.0 * depth / depth_count
+        h_next = 1.0 + (2.0 * depth + 1.0) / depth_count
+        for y in range(0, rows, 8):
+            at = pl.ds(pl.multiple_of(z * rows + y, 8), 8)
+            word = links[at, :]
+            alive = active[at, :].astype(F32)
+
+            def faces(k, h):
+                return jnp.where(jnp.bitwise_and(word, 2**k) != 0, h, 0.0)
+
+            is_active[at, :] = alive
+            face_small[at, :] = alive * h_here
+            face_z[at, :] = faces(1, h_next)
+            face_y[at, :] = faces(3, h_here)
+            face_x[at, :] = faces(5, h_here)
+            if y == 0:
+                first_y[pl.ds(pl.multiple_of(z * 8, 8), 8), :] = faces(2, h_here)
+        return c
+
+    lax.fori_loop(0, layers, prepare, 0)
+    for y in range(0, rows, 8):
+        word = links[y : y + 8, :]
+        first_z[y : y + 8, :] = jnp.where(
+            jnp.bitwise_and(word, 1) != 0, 1.0 + (2.0 * z_base - 1.0) / depth_count, 0.0
+        )
+
+    load_model.wait()
+
     def mask_model(b, c):
-        model[b] = model[b] * row_of(active, b).astype(F32)
+        model[b] = model[b] * row_of(is_active, b)
         return c
 
     lax.fori_loop(0, cells, mask_model, 0, unroll=8)
@@ -135,15 +221,28 @@
     up_y = (region, (survey + 1) % surveys)
     down_y = (region, (survey + surveys - 1) % surveys)
 
-    def send_halo(field, into_z, into_y, base, stage):
+    def send_halo(field, into_z, into_y, base):
         for z in range(layers):
-            stage_y[stage, 0, z] = field[z * rows]
-            stage_y[stage, 1, z] = field[z * rows + rows - 1]
+            stage_y[0, z] = field[z * rows]
+            stage_y[1, z] = field[z * rows + rows - 1]
         last = (layers - 1) * rows
         remote(field.at[pl.ds(0, rows)], into_z.at[1], base, down_z).start()
         remote(field.at[pl.ds(last, rows)], into_z.at[0], base + 1, up_z).start()
-        remote(stage_y.at[stage, 0], into_y.at[1], base + 2, down_y).start()
-        remote(stage_y.at[stage, 1], into_y.at[0], base + 3, up_y).start()
+        remote(stage_y.at[0], into_y.at[1], base + 2, down_y).start()
+        remote(stage_y.at[1], into_y.at[0], base + 3, up_y).start()
+
+    def send_grad_halo(base, side, stage):
+        for y in range(rows):
+            stage_grad_z[stage, y] = grad[side * (layers - 1) * rows + y].astype(BF16)
+        for z in range(layers):
+            stage_grad_y[stage, z] = grad[z * rows + side * (rows - 1)].astype(BF16)
+        to_z, to_y = (up_z, up_y) if side else (down_z, down_y)
+        remote(stage_grad_z.at[stage], grad_z.at[stage], base, to_z).start()
+        remote(stage_grad_y.at[stage], grad_y.at[stage], base + 1, to_y).start()
+
+    def await_grad_halo(sems, base, stage):
+        await_bytes(grad_z.at[stage], sems.at[base])
+        await_bytes(grad_y.at[stage], sems.at[base + 1])
 
     def await_halo(into_z, into_y, base):
         await_bytes(into_z.at[1], recv_sem.at[base])
@@ -151,18 +250,18 @@
         await_bytes(into_y.at[1], recv_sem.at[base + 2])
         await_bytes(into_y.at[0], recv_sem.at[base + 3])
 
-    def sent_halo(field, base, stage):
+    def sent_halo(field, base):
         await_bytes(field.at[pl.ds(0, rows)], send_sem.at[base])
         await_bytes(field.at[pl.ds(0, rows)], send_sem.at[base + 1])
-        await_bytes(stage_y.at[stage, 0], send_sem.at[base + 2])
-        await_bytes(stage_y.at[stage, 1], send_sem.at[base + 3])
-
-    send_halo(model, halo_z, halo_y, 10, 0)
+        await_bytes(stage_y.at[0], send_sem.at[base + 2])
+        await_bytes(stage_y.at[1], send_sem.at[base + 3])
+
+    send_halo(model, halo_z, halo_y, 10)
 
     await_bytes(asked.at[pl.ds(0, owners - 1)], recv_sem.at[0])
-    to_scalar = pltpu.make_async_copy(asked, asked_s, load_sem.at[2])
-    to_scalar.start()
-    to_scalar.wait()
+    load(asked, asked_s, 8).wait()
+    load_slots.wait()
+    load_entries.wait()
 
     def exchange(number, first_of, second_of):
         def send(i, c):
@@ -189,8 +288,8 @@
     def give_back(number):
         exchange(
             number,
-            lambda to: product[entry_of[2 * to]].astype(BF16),
-            lambda to: product[entry_of[2 * to + 1]].astype(BF16),
+            lambda to: product[entry_of[0, to]].astype(BF16),
+            lambda to: product[entry_of[1, to]].astype(BF16),
         )
 
     def await_round(number):
@@ -212,42 +311,26 @@
     for s in range(8):
         scale = jnp.where(sample == s, reg_weight[s], scale)
 
-    def bit(word, k):
-        return ((word // 2**k) % 2).astype(F32)
-
     def regularize():
-        def flux(difference, link):
-            weight = link * lax.rsqrt(difference * difference + EPS_SQ)
+        def flux(difference, face):
+            weight = face * lax.rsqrt(difference * difference + EPS_SQ)
             return weight, weight * difference
 
-        z_base = (region * layers).astype(F32)
         for y in range(rows):
-            link = bit(row_of(links, y), 0) * (1.0 + (2.0 * z_base - 1.0) / depth_count)
-            low_z[y] = flux(model[y] - halo_z[0, y], link)[1]
+            low_z[y] = flux(model[y] - halo_z[0, y], row_of(first_z, y))[1]
 
         def one_layer(z, c, last):
-            depth = z_base + (z if last else z.astype(F32))
-            h_here = 1.0 + 2.0 * depth / depth_count
-            h_next = 1.0 + (2.0 * depth + 1.0) / depth_count
             first = model[z * rows]
-            _, before = flux(
-                first - halo_y[0, z], bit(row_of(links, z * rows), 2) * h_here
-            )
+            _, before = flux(first - halo_y[0, z], row_of(first_y, z * 8))
             for y in range(rows):
                 b = z * rows + y
                 here = model[b]
-                if last:
-                    above = halo_z[1, y]
-                else:
-                    above = model[b + rows]
+                above = halo_z[1, y] if last else model[b + rows]
                 beside = model[b + 1] if y < rows - 1 else halo_y[1, z]
-                word = row_of(links, b)
-                small = (
-                    row_of(active, b).astype(F32) * h_here * lax.rsqrt(here * here + EPS_SQ)
-                )
-                wz, fz = flux(above - here, bit(word, 1) * h_next)
-                wy, fy = flux(beside - here, bit(word, 3) * h_here)
-                wx, fx = flux(pltpu.roll(here, 127, 1) - here, bit(word, 5) * h_here)
+                small = row_of(face_small, b) * lax.rsqrt(here * here + EPS_SQ)
+                wz, fz = flux(above - here, row_of(face_z, b))
+                wy, fy = flux(beside - here, row_of(face_y, b))
+                wx, fx = flux(pltpu.roll(here, 127, 1) - here, row_of(face_x, b))
                 total = (
                     small * here
                     + (low_z[y] - fz)
@@ -273,10 +356,10 @@
                 b = z * rows + y
                 here = grad[b]
                 if last:
-                    above = grad_z[after, y]
+                    above = grad_z[after, y].astype(F32)
                 else:
                     above = grad[b + rows]
-                beside = grad[b + 1] if y < rows - 1 else grad_y[after, z]
+                beside = grad[b + 1] if y < rows - 1 else grad_y[after, z].astype(F32)
                 dz, dy, dx = above - here, beside - here, pltpu.roll(here, 127, 1) - here
                 square = here * here
                 norm = norm + square
@@ -296,27 +379,25 @@
             jnp.sum(curv * scale, axis=1, keepdims=True),
         )
 
-    def pick(number):
-        def one(e, c):
-            t, column = e // width, e % width
-            at = pl.ds(pl.multiple_of(column * 128, 128), 128)
-            picked[t, :, at] = came[number][slot_of[e]].astype(F32)
-            return c
-
-        lax.fori_loop(0, tiles * width, one, 0, unroll=4)
-
-    def forward(t):
-        chunk = 1024
-        total = jnp.zeros((8, slots), F32)
-        for c in range(width * 128 // chunk):
-            at = slice(c * chunk, (c + 1) * chunk)
-            total = total + lax.dot_general(
-                picked[t, :, at].astype(BF16),
-                sens[t, :, at],
-                (((1,), (1,)), ((), ())),
-                preferred_element_type=F32,
+    def forward(t, number):
+        for e in range(width):
+            picked[t, :, e * 128 : (e + 1) * 128] = came[number][
+                slot_of[0, t * width + e]
+            ].astype(F32)
+        these = picked[t].astype(BF16)
+        block = 256
+        made = [
+            jnp.transpose(
+                lax.dot_general(
+                    sens[t, d : d + block, :],
+                    these,
+                    (((1,), (1,)), ((), ())),
+                    preferred_element_type=F32,
+                )
             )
-        return total
+            for d in range(0, slots, block)
+        ]
+        return jnp.concatenate(made, axis=1)
 
     def backward(t, weighted):
         chunk = 1024
@@ -361,7 +442,7 @@
                 data_grad[b] = total
             else:
                 total = data_grad[b] - step * total
-            grad[b] = row_of(active, b).astype(F32) * total + reg_part[b]
+            grad[b] = row_of(is_active, b) * total + reg_part[b]
             return c
 
         lax.fori_loop(0, cells, one, 0, unroll=8)
@@ -379,7 +460,7 @@
 
         lax.fori_loop(1, surveys, send, 0)
 
-    def sum_end(number):
+    def sum_middle(number):
         await_bytes(sum_a.at[number, pl.ds(0, surveys - 1)], recv_sem.at[6 + 2 * number])
         part = sum_a[number, 0]
         for i in range(1, surveys):
@@ -395,6 +476,8 @@
             return c
 
         lax.fori_loop(1, regions, send, 0)
+
+    def sum_end(number):
         await_bytes(sum_b.at[number, pl.ds(0, regions - 1)], recv_sem.at[7 + 2 * number])
         whole = sum_b[number, 0]
         for i in range(1, regions):
@@ -409,42 +492,38 @@
     await_halo(halo_z, halo_y, 10)
     regularize()
     load_sens.wait()
+    load_observed.wait()
+    load_weight.wait()
 
     await_round(1)
-    pick(1)
-
-    def first_pass(t, c):
-        gap = forward(t) - observed[t]
+    for t in range(tiles):
+        gap = forward(t, 1) - observed[t]
         residual[t] = gap
         backward(t, (weight_of(t) * gap).astype(BF16))
-        return c
-
-    lax.fori_loop(0, tiles, first_pass, 0)
     give_back(2)
     await_round(2)
     scatter(2)
     make_gradient(None)
+    send_grad_halo(14, 0, 0)
+    send_grad_halo(16, 1, 1)
     fetch(grad, 3)
-    send_halo(grad, grad_z, grad_y, 14, 1)
-    await_halo(grad_z, grad_y, 14)
-    norm, reg_curv = curvature(1)
+    await_grad_halo(recv_sem, 14, 0)
+    await_grad_halo(recv_sem, 16, 1)
+    norm, reg_curv = curvature(0)
 
     await_round(3)
-    pick(3)
-
-    def second_pass(t, total):
-        made = forward(t)
+    data_curv = jnp.zeros((8, 1), F32)
+    for t in range(tiles):
+        made = forward(t, 3)
         step_pred[t] = made
-        scaled = weight_of(t) * made
-        backward(t, scaled.astype(BF16))
-        return total + jnp.sum(scaled * made, axis=1, keepdims=True)
-
-    data_curv = lax.fori_loop(0, tiles, second_pass, jnp.zeros((8, 1), F32))
+        data_curv = data_curv + jnp.sum(weight_of(t) * made * made, axis=1, keepdims=True)
     sum_start(my_sums(norm, reg_curv, data_curv), 0)
+    for t in range(tiles):
+        backward(t, (weight_of(t) * step_pred[t]).astype(BF16))
+    sum_middle(0)
     give_back(4)
     step = sum_end(0)
-    sent_halo(model, 10, 0)
-    sent_halo(grad, 14, 1)
+    sent_halo(model, 10)
     step_row = jnp.broadcast_to(step, (8, 128))
 
     def move(b, c):
@@ -454,52 +533,36 @@
     lax.fori_loop(0, cells, move, 0, unroll=8)
     for side in range(2):
         for y in range(rows):
-            halo_z[side, y] = halo_z[side, y] - step_row * grad_z[side, y]
+            halo_z[side, y] = halo_z[side, y] - step_row * grad_z[1 - side, y].astype(F32)
         for z in range(layers):
-            halo_y[side, z] = halo_y[side, z] - step_row * grad_y[side, z]
-    save_model = pltpu.make_async_copy(model, model_out, load_sem.at[3])
-    save_model.start()
+            halo_y[side, z] = halo_y[side, z] - step_row * grad_y[1 - side, z].astype(F32)
+    save_model = load(model, model_out, 9)
     regularize()
-
-    def move_gap(t, c):
+    for t in range(tiles):
         residual[t] = residual[t] - step * step_pred[t]
-        return c
-
-    lax.fori_loop(0, tiles, move_gap, 0)
 
     await_round(4)
     scatter(4)
     make_gradient(step_row)
+    send_grad_halo(18, 0, 2)
     fetch(grad, 5)
-    save_grad = pltpu.make_async_copy(grad, grad_out, load_sem.at[4])
-    save_grad.start()
-    for z in range(layers):
-        stage_y[2, 0, z] = grad[z * rows]
-    remote(grad.at[pl.ds(0, rows)], grad_z.at[2], 18, down_z).start()
-    remote(stage_y.at[2, 0], grad_y.at[2], 19, down_y).start()
-    await_bytes(grad_z.at[2], recv_sem.at[18])
-    await_bytes(grad_y.at[2], recv_sem.at[19])
+    save_grad = load(grad, grad_out, 10)
+    await_grad_halo(recv_sem, 18, 2)
     norm, reg_curv = curvature(2)
 
     await_round(5)
-    pick(5)
-
-    def third_pass(t, total):
-        made = forward(t)
+    data_curv = jnp.zeros((8, 1), F32)
+    for t in range(tiles):
+        made = forward(t, 5)
         step_pred[t] = made
-        return total + jnp.sum(weight_of(t) * made * made, axis=1, keepdims=True)
-
-    data_curv = lax.fori_loop(0, tiles, third_pass, jnp.zeros((8, 1), F32))
+        data_curv = data_curv + jnp.sum(weight_of(t) * made * made, axis=1, keepdims=True)
     sum_start(my_sums(norm, reg_curv, data_curv), 1)
+    sum_middle(1)
     step = sum_end(1)
     step_out[...] = jnp.broadcast_to(step, (8, 128))
-
-    def finish(t, c):
+    for t in range(tiles):
         weight = mask_of(t) * data_weight[pl.ds(t, 1), :]
         misfit_out[t] = weight * (residual[t] - step * step_pred[t])
-        return c
-
-    lax.fori_loop(0, tiles, finish, 0)
 
     await_bytes(ask.at[pl.ds(0, owners - 1)], send_sem.at[0])
     for number in range(1, 6):
@@ -507,10 +570,28 @@
     for number in range(2):
         await_bytes(sum_a.at[number, pl.ds(0, surveys - 1)], send_sem.at[6 + 2 * number])
         await_bytes(sum_b.at[number, pl.ds(0, regions - 1)], send_sem.at[7 + 2 * number])
-    await_bytes(grad.at[pl.ds(0, rows)], send_sem.at[18])
-    await_bytes(stage_y.at[2, 0], send_sem.at[19])
+    for stage in range(3):
+        await_grad_halo(send_sem, 14 + 2 * stage, stage)
     save_model.wait()
     save_grad.wait()
+
+
+def finish(moved, gradient, step, misfit, final_out, misfit_out, made, sem):
+    parts = made.shape[0]
+    size = made.shape[1]
+    copy_misfit = pltpu.make_async_copy(misfit, misfit_out, sem.at[parts])
+    copy_misfit.start()
+    copies = []
+    for i in range(parts):
+        for b in range(size):
+            made[i, b] = moved[i * size + b] - step[...] * gradient[i * size + b]
+        copies.append(
+            pltpu.make_async_copy(made.at[i], final_out.at[pl.ds(i * size, size)], sem.at[i])
+        )
+        copies[-1].start()
+    for copy in copies:
+        copy.wait()
+    copy_misfit.wait()
 
 
 def shards(
@@ -532,26 +613,15 @@
     owners, cells = regions * surveys, layers * rows
     entries = tiles * width
 
-    wanted = tile_bricks.reshape(entries)
-    owner_of, local_of = wanted // cells, wanted % cells
-    number = jnp.arange(entries, dtype=jnp.int32)
-    earlier = (owner_of[:, None] == owner_of[None, :]) & (number[None, :] < number[:, None])
-    rank_of = jnp.sum(earlier.astype(jnp.int32), axis=1)
-    slot_of = 2 * owner_of + rank_of
-    hits = jnp.arange(2 * owners, dtype=jnp.int32)[:, None] == slot_of[None, :]
-    ask = jnp.sum(jnp.where(hits, local_of[None, :] + 1, 0), axis=1) - 1
-    entry_of = jnp.sum(jnp.where(hits, number[None, :], 0), axis=1)
-    ask = ask.reshape(owners, 1, 2)
-    ask = jnp.concatenate([jnp.maximum(ask, 0), ask], axis=2)
-    ask = jnp.pad(ask, ((0, 0), (0, 0), (0, 124)))
-
     field = jax.ShapeDtypeStruct((cells, samples, across), F32)
     field_scratch = pltpu.VMEM(field.shape, F32)
     blocks = pltpu.VMEM((2 * owners, samples, across), BF16)
     data_scratch = pltpu.VMEM((tiles, samples, slots), F32)
+    plane = pltpu.VMEM((cells, across), F32)
     vmem = pl.BlockSpec(memory_space=pltpu.VMEM)
     smem = pl.BlockSpec(memory_space=pltpu.SMEM)
     anywhere = pl.BlockSpec(memory_space=pl.ANY)
+    in_hbm = pl.BlockSpec(memory_space=pltpu.HBM)
     moved, gradient, step, misfit = pl.pallas_call(
         functools.partial(kernel, (regions, surveys, layers, rows, tiles, width, slots)),
         name="inversion",
@@ -561,7 +631,7 @@
             jax.ShapeDtypeStruct((samples, across), F32),
             jax.ShapeDtypeStruct((tiles, samples, slots), F32),
         ),
-        in_specs=[smem] * 4 + [vmem] * 5 + [anywhere] * 2,
+        in_specs=[smem] * 2 + [vmem] + [in_hbm] * 6,
         out_specs=(anywhere, anywhere, vmem, vmem),
         scratch_shapes=[
             pltpu.VMEM(sensitivity.shape, BF16),
@@ -570,47 +640,75 @@
             field_scratch,
             pltpu.VMEM((cells * samples, across), F32),
             *[field_scratch] * 5,
+            pltpu.VMEM(observed.shape, F32),
+            pltpu.VMEM(data_weight.shape, F32),
+            pltpu.VMEM((cells, across), jnp.int32),
+            pltpu.VMEM((cells, across), jnp.int32),
+            *[plane] * 5,
+            pltpu.VMEM((rows, across), F32),
+            pltpu.VMEM((layers * 8, across), F32),
             pltpu.VMEM((rows, 8, 128), F32),
             pltpu.VMEM((owners, 1, 128), jnp.int32),
+            pltpu.VMEM((owners, 1, 128), jnp.int32),
             pltpu.SMEM((owners, 1, 128), jnp.int32),
+            pltpu.VMEM((1, entries), jnp.int32),
+            pltpu.VMEM((2, owners), jnp.int32),
+            pltpu.SMEM((1, entries), jnp.int32),
+            pltpu.SMEM((2, owners), jnp.int32),
             pltpu.VMEM((tiles, samples, width * 128), F32),
             pltpu.VMEM((entries, samples, across), F32),
-            data_scratch,
             data_scratch,
             data_scratch,
             *[blocks] * 10,
             pltpu.VMEM((owners * 16, 128), F32),
             pltpu.VMEM((cells, 2 * owners), BF16),
-            pltpu.VMEM((3, 2, layers, 8, 128), F32),
+            pltpu.VMEM((2, layers, 8, 128), F32),
+            pltpu.VMEM((3, rows, 8, 128), BF16),
+            pltpu.VMEM((3, layers, 8, 128), BF16),
             pltpu.VMEM((2, rows, 8, 128), F32),
             pltpu.VMEM((2, layers, 8, 128), F32),
-            pltpu.VMEM((3, rows, 8, 128), F32),
-            pltpu.VMEM((3, layers, 8, 128), F32),
+            pltpu.VMEM((3, rows, 8, 128), BF16),
+            pltpu.VMEM((3, layers, 8, 128), BF16),
             pltpu.VMEM((2, 2, 8, 128), F32),
             pltpu.VMEM((2, surveys, 8, 128), F32),
             pltpu.VMEM((2, regions, 8, 128), F32),
-            pltpu.SemaphoreType.DMA((5,)),
+            pltpu.SemaphoreType.DMA((12,)),
             pltpu.SemaphoreType.DMA((20,)),
             pltpu.SemaphoreType.DMA((20,)),
         ],
         compiler_params=pltpu.CompilerParams(
-            collective_id=0, has_side_effects=True, vmem_limit_bytes=60 << 20
+            collective_id=0, has_side_effects=True, vmem_limit_bytes=49 << 20
         ),
     )(
-        slot_of,
-        entry_of,
-        data_counts,
-        reg_weight,
-        ask,
-        observed,
-        data_weight,
-        active_cells.reshape(cells, across),
-        face_links.reshape(cells, across),
-        start_model.reshape(cells, samples, across),
-        sensitivity,
+        *(
+            pltpu.with_memory_space_constraint(x, pltpu.HBM)
+            for x in (
+                data_counts,
+                reg_weight,
+                tile_bricks,
+                observed,
+                data_weight,
+                active_cells.reshape(cells, across),
+                face_links.reshape(cells, across),
+                start_model.reshape(cells, samples, across),
+                sensitivity,
+            )
+        )
     )
-    final = moved.reshape(start_model.shape) - step * gradient.reshape(start_model.shape)
-    return final, misfit
+    parts = 8
+    final, misfit = pl.pallas_call(
+        finish,
+        name="finish",
+        out_shape=(field, jax.ShapeDtypeStruct(misfit.shape, F32)),
+        in_specs=[vmem] * 4,
+        out_specs=(in_hbm, in_hbm),
+        scratch_shapes=[
+            pltpu.VMEM((parts, cells // parts, samples, across), F32),
+            pltpu.SemaphoreType.DMA((parts + 1,)),
+        ],
+        compiler_params=pltpu.CompilerParams(vmem_limit_bytes=8 << 20),
+    )(moved, gradient, step, misfit)
+    return final.reshape(start_model.shape), misfit
 
 
 def solution(mesh):

time: 132 us -> 107 us (0.81)
  Pallas kernels: 124 us -> 106 us
  other arithmetic: 5.06 us -> 0 us
  local copies, waits for them, and re-layouts: 2.22 us -> 0 us
    pallas_call x1, Pallas kernels: 124 us -> 105 us  [shards(): pl.pallas_call(functools.partial(kernel, (regions, surveys, layers, rows,...]
    sub x2 -> x0, other arithmetic: 3.87 us -> none  [the longest x1 3.86 us: shards(): moved.reshape(start_model.shape)]
    pallas_call x0 -> x1, Pallas kernels: none -> 1.42 us  [shards(): pl.pallas_call(finish, name='finish', out_shape=(field, jax.ShapeDtypeStr...]
where the time goes in v2:
time: 107 us
  Pallas kernels  106 us (99%)
    pallas_call x1, Pallas kernels, shards(): pl.pallas_call(functools.partial(kernel, (regions, surveys, layers, rows,...  105 us

profile of v2, /device:TPU:1, one launch (start us, length us, event | category | flops | bytes accessed | tf_op | source)
XLA Modules:
  0.0 107.2 jit_solution(11709851960567905788)
XLA Ops:
  0.6 105.0 %inversion.1 = (f32[512,8,128]{2,1,0:T(8,128)S(1)}, f32[512,8,128]{2,1,0:T(8,128)S(1)}, f32[8,128]{1,0:T(8,128)S(1)}, f32[4,8,512]{2,1,0:T(8,128)S(1)}) custom-call(s32[4]{0:T(128)} %counts.1, f32[8]{0:T(128)} %reg_weight.1, s32[4,32]{1,0:T(4,128)} %bricks.1, f32[4,8,512]{2,1,0:T(8,128)} %observed_hbm.1, f32[4,512]{1,0:T(4,128)} %data_weight_hbm.1, ...), custom_call_target="tpu_custom_call" | custom-call | tf_op jit(solution)/shard_map/inversion/pallas_call | solution.py:625
  105.6 1.4 %finish.1 = (f32[512,8,128]{2,1,0:T(8,128)}, f32[4,8,512]{2,1,0:T(8,128)}) custom-call(f32[512,8,128]{2,1,0:T(8,128)S(1)} %get-tuple-element.8.moved, f32[512,8,128]{2,1,0:T(8,128)S(1)} %get-tuple-element.9.gradient, f32[8,128]{1,0:T(8,128)S(1)} %get-tuple-element.10.step, f32[4,8,512]{2,1,0:T(8,128)S(1)} %get-tuple-element.11.misfit), custom_call_target="tpu_custom_call" | custom-call | tf_op jit(solution)/shard_map/finish/pallas_call | solution.py:699

commit v3 on v2

--- a/solution.py
+++ b/solution.py
@@ -28,15 +28,11 @@
     step_out,
     misfit_out,
     sens,
+    sens_t,
     model,
     grad,
-    data_grad,
     sums,
     reg_part,
-    w_small,
-    w_z,
-    w_y,
-    w_x,
     observed,
     data_weight,
     active,
@@ -51,6 +47,7 @@
     low_z,
     ask,
     asked,
+    asked_rows,
     asked_s,
     slot_row,
     entry_rows,
@@ -62,14 +59,8 @@
     step_pred,
     sent1,
     sent2,
-    sent3,
-    sent4,
-    sent5,
     came1,
     came2,
-    came3,
-    came4,
-    came5,
     spread,
     one_hot,
     stage_y,
@@ -96,8 +87,8 @@
     def device(flat):
         return (flat // surveys, flat % surveys)
 
-    sent = (None, sent1, sent2, sent3, sent4, sent5)
-    came = (None, came1, came2, came3, came4, came5)
+    sent = (sent2, sent1) * 3
+    came = (came2, came1) * 3
     barrier = pltpu.get_barrier_semaphore()
 
     def greet(i, c):
@@ -117,7 +108,7 @@
     load_model = load(model_hbm, model, 2)
     load_observed = load(observed_hbm, observed, 3)
     load_weight = load(data_weight_hbm, data_weight, 4)
-    load_sens = load(sens_hbm, sens, 5)
+    load_sens = [load(sens_hbm.at[t], sens.at[t], 5 + t) for t in range(tiles)]
 
     entries = tiles * width
     wanted = jnp.concatenate([bricks[t : t + 1, :] for t in range(tiles)], axis=1)
@@ -147,8 +138,8 @@
         table = jnp.where(across == 2 + rank, number, table)
         entry_rows[rank : rank + 1, :] = count(theirs & (rank_col == rank), upright, 0)
     ask[...] = table.reshape(owners, 1, 128)
-    load_slots = load(slot_row, slot_of, 6)
-    load_entries = load(entry_rows, entry_of, 7)
+    load_slots = load(slot_row, slot_of, 9)
+    load_entries = load(entry_rows, entry_of, 10)
     pl.semaphore_wait(barrier, owners - 1)
 
     def remote(src, dst, number, to):
@@ -258,8 +249,23 @@
 
     send_halo(model, halo_z, halo_y, 10)
 
+    def turn(t):
+        load_sens[t].wait()
+
+        def one(c, carry):
+            at = pl.ds(pl.multiple_of(c * 512, 512), 512)
+            sens_t[t, at, :] = jnp.transpose(sens[t, :, at])
+            return carry
+
+        lax.fori_loop(0, width * 128 // 512, one, 0)
+
+    turn(0)
+    turn(1)
+
     await_bytes(asked.at[pl.ds(0, owners - 1)], recv_sem.at[0])
-    load(asked, asked_s, 8).wait()
+    ids = jnp.transpose(asked[:, 0, :])
+    asked_rows[...] = ids[0:2, :]
+    load(asked_rows, asked_s, 11).wait()
     load_slots.wait()
     load_entries.wait()
 
@@ -274,6 +280,8 @@
             ).start()
             return c
 
+        if number > 2:
+            await_bytes(sent[number].at[pl.ds(0, 2 * owners - 2)], send_sem.at[number - 2])
         lax.fori_loop(1, owners, send, 0)
         came[number][2 * me] = first_of(me)
         came[number][2 * me + 1] = second_of(me)
@@ -281,8 +289,8 @@
     def fetch(field, number):
         exchange(
             number,
-            lambda to: field[asked_s[to, 0, 0]].astype(BF16),
-            lambda to: field[asked_s[to, 0, 1]].astype(BF16),
+            lambda to: field[asked_s[0, to]].astype(BF16),
+            lambda to: field[asked_s[1, to]].astype(BF16),
         )
 
     def give_back(number):
@@ -297,8 +305,7 @@
 
     fetch(model, 1)
 
-    ids = jnp.transpose(asked[:, 0, :].astype(F32))
-    numbers = lax.broadcasted_iota(jnp.int32, (cells, owners), 0).astype(F32)
+    numbers = lax.broadcasted_iota(jnp.int32, (cells, owners), 0)
     for rank in range(2):
         named = jnp.broadcast_to(ids[2 + rank : 3 + rank, :], (cells, owners))
         one_hot[:, rank * owners : (rank + 1) * owners] = jnp.where(
@@ -311,37 +318,38 @@
     for s in range(8):
         scale = jnp.where(sample == s, reg_weight[s], scale)
 
-    def regularize():
+    def conduct(difference, face):
+        return face * lax.rsqrt(difference * difference + EPS_SQ)
+
+    def regularize(data_part):
         def flux(difference, face):
-            weight = face * lax.rsqrt(difference * difference + EPS_SQ)
-            return weight, weight * difference
+            return conduct(difference, face) * difference
 
         for y in range(rows):
-            low_z[y] = flux(model[y] - halo_z[0, y], row_of(first_z, y))[1]
+            low_z[y] = flux(model[y] - halo_z[0, y], row_of(first_z, y))
 
         def one_layer(z, c, last):
             first = model[z * rows]
-            _, before = flux(first - halo_y[0, z], row_of(first_y, z * 8))
+            before = flux(first - halo_y[0, z], row_of(first_y, z * 8))
             for y in range(rows):
                 b = z * rows + y
                 here = model[b]
                 above = halo_z[1, y] if last else model[b + rows]
                 beside = model[b + 1] if y < rows - 1 else halo_y[1, z]
-                small = row_of(face_small, b) * lax.rsqrt(here * here + EPS_SQ)
-                wz, fz = flux(above - here, row_of(face_z, b))
-                wy, fy = flux(beside - here, row_of(face_y, b))
-                wx, fx = flux(pltpu.roll(here, 127, 1) - here, row_of(face_x, b))
+                small = conduct(here, row_of(face_small, b))
+                fz = flux(above - here, row_of(face_z, b))
+                fy = flux(beside - here, row_of(face_y, b))
+                fx = flux(pltpu.roll(here, 127, 1) - here, row_of(face_x, b))
                 total = (
                     small * here
                     + (low_z[y] - fz)
                     + (before - fy)
                     + (pltpu.roll(fx, 1, 1) - fx)
                 )
-                reg_part[b] = scale * total
-                w_small[b] = small
-                w_z[b] = wz
-                w_y[b] = wy
-                w_x[b] = wx
+                total = scale * total
+                if data_part:
+                    total = total + (grad[b] - reg_part[b])
+                reg_part[b] = total
                 low_z[y] = fz
                 before = fy
             return c
@@ -349,24 +357,26 @@
         lax.fori_loop(0, layers - 1, functools.partial(one_layer, last=False), 0)
         one_layer(layers - 1, 0, True)
 
-    def curvature(after):
+    def curvature(after, base):
         def one_layer(z, carry, last):
             norm, curv = carry
             for y in range(rows):
                 b = z * rows + y
-                here = grad[b]
-                if last:
-                    above = grad_z[after, y].astype(F32)
-                else:
-                    above = grad[b + rows]
-                beside = grad[b + 1] if y < rows - 1 else grad_y[after, z].astype(F32)
-                dz, dy, dx = above - here, beside - here, pltpu.roll(here, 127, 1) - here
+                here, cell = grad[b], model[b]
                 square = here * here
                 norm = norm + square
-                curv = curv + (
-                    (w_small[b] * square + w_z[b] * (dz * dz))
-                    + (w_y[b] * (dy * dy) + w_x[b] * (dx * dx))
-                )
+                dx = pltpu.roll(here, 127, 1) - here
+                part = conduct(cell, row_of(face_small, b)) * square
+                part = part + conduct(
+                    pltpu.roll(cell, 127, 1) - cell, row_of(face_x, b)
+                ) * (dx * dx)
+                if not last:
+                    dz = grad[b + rows] - here
+                    part = part + conduct(model[b + rows] - cell, row_of(face_z, b)) * (dz * dz)
+                if y < rows - 1:
+                    dy = grad[b + 1] - here
+                    part = part + conduct(model[b + 1] - cell, row_of(face_y, b)) * (dy * dy)
+                curv = curv + part
             return norm, curv
 
         zero = jnp.zeros((8, 128), F32)
@@ -374,6 +384,15 @@
             0, layers - 1, functools.partial(one_layer, last=False), (zero, zero)
         )
         norm, curv = one_layer(layers - 1, carry, True)
+        await_grad_halo(recv_sem, base, after)
+        for y in range(rows):
+            b = (layers - 1) * rows + y
+            dz = grad_z[after, y].astype(F32) - grad[b]
+            curv = curv + conduct(halo_z[1, y] - model[b], row_of(face_z, b)) * (dz * dz)
+        for z in range(layers):
+            b = z * rows + rows - 1
+            dy = grad_y[after, z].astype(F32) - grad[b]
+            curv = curv + conduct(halo_y[1, z] - model[b], row_of(face_y, b)) * (dy * dy)
         return (
             jnp.sum(norm, axis=1, keepdims=True),
             jnp.sum(curv * scale, axis=1, keepdims=True),
@@ -384,20 +403,7 @@
             picked[t, :, e * 128 : (e + 1) * 128] = came[number][
                 slot_of[0, t * width + e]
             ].astype(F32)
-        these = picked[t].astype(BF16)
-        block = 256
-        made = [
-            jnp.transpose(
-                lax.dot_general(
-                    sens[t, d : d + block, :],
-                    these,
-                    (((1,), (1,)), ((), ())),
-                    preferred_element_type=F32,
-                )
-            )
-            for d in range(0, slots, block)
-        ]
-        return jnp.concatenate(made, axis=1)
+        return jnp.dot(picked[t].astype(BF16), sens_t[t], preferred_element_type=F32)
 
     def backward(t, weighted):
         chunk = 1024
@@ -437,12 +443,8 @@
 
     def make_gradient(step):
         def one(b, c):
-            total = sums[pl.ds(pl.multiple_of(b * 8, 8), 8), :]
-            if step is None:
-                data_grad[b] = total
-            else:
-                total = data_grad[b] - step * total
-            grad[b] = row_of(is_active, b) * total + reg_part[b]
+            total = row_of(is_active, b) * sums[pl.ds(pl.multiple_of(b * 8, 8), 8), :]
+            grad[b] = reg_part[b] + total if step is None else reg_part[b] - step * total
             return c
 
         lax.fori_loop(0, cells, one, 0, unroll=8)
@@ -490,8 +492,9 @@
         return jnp.where(lane == 0, norm, jnp.where(lane == 1, reg_curv + data_curv, 0.0))
 
     await_halo(halo_z, halo_y, 10)
-    regularize()
-    load_sens.wait()
+    regularize(False)
+    turn(2)
+    turn(3)
     load_observed.wait()
     load_weight.wait()
 
@@ -505,13 +508,11 @@
     scatter(2)
     make_gradient(None)
     send_grad_halo(14, 0, 0)
+    fetch(grad, 3)
+    norm, reg_curv = curvature(0, 14)
+
+    await_round(3)
     send_grad_halo(16, 1, 1)
-    fetch(grad, 3)
-    await_grad_halo(recv_sem, 14, 0)
-    await_grad_halo(recv_sem, 16, 1)
-    norm, reg_curv = curvature(0)
-
-    await_round(3)
     data_curv = jnp.zeros((8, 1), F32)
     for t in range(tiles):
         made = forward(t, 3)
@@ -531,13 +532,14 @@
         return c
 
     lax.fori_loop(0, cells, move, 0, unroll=8)
+    await_grad_halo(recv_sem, 16, 1)
     for side in range(2):
         for y in range(rows):
             halo_z[side, y] = halo_z[side, y] - step_row * grad_z[1 - side, y].astype(F32)
         for z in range(layers):
             halo_y[side, z] = halo_y[side, z] - step_row * grad_y[1 - side, z].astype(F32)
-    save_model = load(model, model_out, 9)
-    regularize()
+    save_model = load(model, model_out, 12)
+    regularize(True)
     for t in range(tiles):
         residual[t] = residual[t] - step * step_pred[t]
 
@@ -546,9 +548,8 @@
     make_gradient(step_row)
     send_grad_halo(18, 0, 2)
     fetch(grad, 5)
-    save_grad = load(grad, grad_out, 10)
-    await_grad_halo(recv_sem, 18, 2)
-    norm, reg_curv = curvature(2)
+    save_grad = load(grad, grad_out, 13)
+    norm, reg_curv = curvature(2, 18)
 
     await_round(5)
     data_curv = jnp.zeros((8, 1), F32)
@@ -565,7 +566,7 @@
         misfit_out[t] = weight * (residual[t] - step * step_pred[t])
 
     await_bytes(ask.at[pl.ds(0, owners - 1)], send_sem.at[0])
-    for number in range(1, 6):
+    for number in range(4, 6):
         await_bytes(sent[number].at[pl.ds(0, 2 * owners - 2)], send_sem.at[number])
     for number in range(2):
         await_bytes(sum_a.at[number, pl.ds(0, surveys - 1)], send_sem.at[6 + 2 * number])
@@ -635,11 +636,11 @@
         out_specs=(anywhere, anywhere, vmem, vmem),
         scratch_shapes=[
             pltpu.VMEM(sensitivity.shape, BF16),
-            field_scratch,
+            pltpu.VMEM((tiles, width * across, slots), BF16),
             field_scratch,
             field_scratch,
             pltpu.VMEM((cells * samples, across), F32),
-            *[field_scratch] * 5,
+            field_scratch,
             pltpu.VMEM(observed.shape, F32),
             pltpu.VMEM(data_weight.shape, F32),
             pltpu.VMEM((cells, across), jnp.int32),
@@ -650,7 +651,8 @@
             pltpu.VMEM((rows, 8, 128), F32),
             pltpu.VMEM((owners, 1, 128), jnp.int32),
             pltpu.VMEM((owners, 1, 128), jnp.int32),
-            pltpu.SMEM((owners, 1, 128), jnp.int32),
+            pltpu.VMEM((2, owners), jnp.int32),
+            pltpu.SMEM((2, owners), jnp.int32),
             pltpu.VMEM((1, entries), jnp.int32),
             pltpu.VMEM((2, owners), jnp.int32),
             pltpu.SMEM((1, entries), jnp.int32),
@@ -659,7 +661,7 @@
             pltpu.VMEM((entries, samples, across), F32),
             data_scratch,
             data_scratch,
-            *[blocks] * 10,
+            *[blocks] * 4,
             pltpu.VMEM((owners * 16, 128), F32),
             pltpu.VMEM((cells, 2 * owners), BF16),
             pltpu.VMEM((2, layers, 8, 128), F32),
@@ -672,12 +674,12 @@
             pltpu.VMEM((2, 2, 8, 128), F32),
             pltpu.VMEM((2, surveys, 8, 128), F32),
             pltpu.VMEM((2, regions, 8, 128), F32),
-            pltpu.SemaphoreType.DMA((12,)),
+            pltpu.SemaphoreType.DMA((14,)),
             pltpu.SemaphoreType.DMA((20,)),
             pltpu.SemaphoreType.DMA((20,)),
         ],
         compiler_params=pltpu.CompilerParams(
-            collective_id=0, has_side_effects=True, vmem_limit_bytes=49 << 20
+            collective_id=0, has_side_effects=True, vmem_limit_bytes=97 << 19
         ),
     )(
         *(

time: 107 us -> 97.3 us (0.909)
  Pallas kernels: 106 us -> 96.6 us
    pallas_call x1, Pallas kernels: 105 us -> 95.2 us  [shards(): pl.pallas_call(functools.partial(kernel, (regions, surveys, layers, rows,...]
where the time goes in v3:
time: 97.3 us
  Pallas kernels  96.6 us (99%)
    pallas_call x1, Pallas kernels, shards(): pl.pallas_call(functools.partial(kernel, (regions, surveys, layers, rows,...  95.2 us

profile of v3, /device:TPU:1, one launch (start us, length us, event | category | flops | bytes accessed | tf_op | source)
XLA Modules:
  0.0 97.3 jit_solution(12882877919863963375)
XLA Ops:
  0.6 95.2 %inversion.1 = (f32[512,8,128]{2,1,0:T(8,128)S(1)}, f32[512,8,128]{2,1,0:T(8,128)S(1)}, f32[8,128]{1,0:T(8,128)S(1)}, f32[4,8,512]{2,1,0:T(8,128)S(1)}) custom-call(s32[4]{0:T(128)} %counts.1, f32[8]{0:T(128)} %reg_weight.1, s32[4,32]{1,0:T(4,128)} %bricks.1, f32[4,8,512]{2,1,0:T(8,128)} %observed_hbm.1, f32[4,512]{1,0:T(4,128)} %data_weight_hbm.1, ...), custom_call_target="tpu_custom_call" | custom-call | tf_op jit(solution)/shard_map/inversion/pallas_call | solution.py:626
  95.8 1.4 %finish.1 = (f32[512,8,128]{2,1,0:T(8,128)}, f32[4,8,512]{2,1,0:T(8,128)}) custom-call(f32[512,8,128]{2,1,0:T(8,128)S(1)} %get-tuple-element.8.moved, f32[512,8,128]{2,1,0:T(8,128)S(1)} %get-tuple-element.9.gradient, f32[8,128]{1,0:T(8,128)S(1)} %get-tuple-element.10.step, f32[4,8,512]{2,1,0:T(8,128)S(1)} %get-tuple-element.11.misfit), custom_call_target="tpu_custom_call" | custom-call | tf_op jit(solution)/shard_map/finish/pallas_call | solution.py:701

commit v4 on v3

--- a/solution.py
+++ b/solution.py
@@ -269,7 +269,7 @@
     load_slots.wait()
     load_entries.wait()
 
-    def exchange(number, first_of, second_of):
+    def exchange(number, first_of, second_of, between=None):
         def send(i, c):
             to = (me + i) % owners
             sent[number][2 * to] = first_of(to)
@@ -282,7 +282,13 @@
 
         if number > 2:
             await_bytes(sent[number].at[pl.ds(0, 2 * owners - 2)], send_sem.at[number - 2])
-        lax.fori_loop(1, owners, send, 0)
+        if between is None:
+            lax.fori_loop(1, owners, send, 0)
+        else:
+            early = 3 * owners // 8
+            lax.fori_loop(1, early, send, 0)
+            between()
+            lax.fori_loop(early, owners, send, 0)
         came[number][2 * me] = first_of(me)
         came[number][2 * me + 1] = second_of(me)
 
@@ -293,11 +299,12 @@
             lambda to: field[asked_s[1, to]].astype(BF16),
         )
 
-    def give_back(number):
+    def give_back(number, between=None):
         exchange(
             number,
             lambda to: product[entry_of[0, to]].astype(BF16),
             lambda to: product[entry_of[1, to]].astype(BF16),
+            between,
         )
 
     def await_round(number):
@@ -357,7 +364,7 @@
         lax.fori_loop(0, layers - 1, functools.partial(one_layer, last=False), 0)
         one_layer(layers - 1, 0, True)
 
-    def curvature(after, base):
+    def curvature():
         def one_layer(z, carry, last):
             norm, curv = carry
             for y in range(rows):
@@ -383,7 +390,9 @@
         carry = lax.fori_loop(
             0, layers - 1, functools.partial(one_layer, last=False), (zero, zero)
         )
-        norm, curv = one_layer(layers - 1, carry, True)
+        return one_layer(layers - 1, carry, True)
+
+    def shared_faces(norm, curv, after, base):
         await_grad_halo(recv_sem, base, after)
         for y in range(rows):
             b = (layers - 1) * rows + y
@@ -433,13 +442,17 @@
 
         lax.fori_loop(0, 2 * owners, widen, 0, unroll=8)
         table = one_hot[...]
-        for s in range(8):
-            first = spread[pl.ds(s, owners, stride=16), :]
-            second = spread[pl.ds(8 + s, owners, stride=16), :]
-            blocks = jnp.concatenate([first, second], axis=0).astype(BF16)
-            sums[pl.ds(s, cells, stride=8), :] = jnp.dot(
-                table, blocks, preferred_element_type=F32
+        for s in range(0, 8, 2):
+            pair = []
+            for sample_row in (s, s + 1):
+                first = spread[pl.ds(sample_row, owners, stride=16), :]
+                second = spread[pl.ds(8 + sample_row, owners, stride=16), :]
+                pair.append(jnp.concatenate([first, second], axis=0).astype(BF16))
+            made = jnp.dot(
+                table, jnp.concatenate(pair, axis=1), preferred_element_type=F32
             )
+            sums[pl.ds(s, cells, stride=8), :] = made[:, :128]
+            sums[pl.ds(s + 1, cells, stride=8), :] = made[:, 128:]
 
     def make_gradient(step):
         def one(b, c):
@@ -507,9 +520,9 @@
     await_round(2)
     scatter(2)
     make_gradient(None)
+    fetch(grad, 3)
     send_grad_halo(14, 0, 0)
-    fetch(grad, 3)
-    norm, reg_curv = curvature(0, 14)
+    inner = curvature()
 
     await_round(3)
     send_grad_halo(16, 1, 1)
@@ -518,11 +531,11 @@
         made = forward(t, 3)
         step_pred[t] = made
         data_curv = data_curv + jnp.sum(weight_of(t) * made * made, axis=1, keepdims=True)
+    norm, reg_curv = shared_faces(*inner, 0, 14)
     sum_start(my_sums(norm, reg_curv, data_curv), 0)
     for t in range(tiles):
         backward(t, (weight_of(t) * step_pred[t]).astype(BF16))
-    sum_middle(0)
-    give_back(4)
+    give_back(4, lambda: sum_middle(0))
     step = sum_end(0)
     sent_halo(model, 10)
     step_row = jnp.broadcast_to(step, (8, 128))
@@ -546,10 +559,10 @@
     await_round(4)
     scatter(4)
     make_gradient(step_row)
+    fetch(grad, 5)
     send_grad_halo(18, 0, 2)
-    fetch(grad, 5)
     save_grad = load(grad, grad_out, 13)
-    norm, reg_curv = curvature(2, 18)
+    inner = curvature()
 
     await_round(5)
     data_curv = jnp.zeros((8, 1), F32)
@@ -557,6 +570,7 @@
         made = forward(t, 5)
         step_pred[t] = made
         data_curv = data_curv + jnp.sum(weight_of(t) * made * made, axis=1, keepdims=True)
+    norm, reg_curv = shared_faces(*inner, 2, 18)
     sum_start(my_sums(norm, reg_curv, data_curv), 1)
     sum_middle(1)
     step = sum_end(1)

time: 97.3 us -> 99 us (1.017)
  Pallas kernels: 96.6 us -> 98.2 us
    pallas_call x1, Pallas kernels: 95.2 us -> 96.8 us  [shards(): pl.pallas_call(functools.partial(kernel, (regions, surveys, layers, rows,...]
where the time goes in v4:
time: 99 us; the launch traced here: 98.8 us
  Pallas kernels  98.2 us (99%)
    pallas_call x1, Pallas kernels, shards(): pl.pallas_call(functools.partial(kernel, (regions, surveys, layers, rows,...  96.8 us

profile of v4, /device:TPU:1, one launch (start us, length us, event | category | flops | bytes accessed | tf_op | source)
XLA Modules:
  0.0 98.8 jit_solution(442426688399044315)
XLA Ops:
  0.6 96.8 %inversion.1 = (f32[512,8,128]{2,1,0:T(8,128)S(1)}, f32[512,8,128]{2,1,0:T(8,128)S(1)}, f32[8,128]{1,0:T(8,128)S(1)}, f32[4,8,512]{2,1,0:T(8,128)S(1)}) custom-call(s32[4]{0:T(128)} %counts.1, f32[8]{0:T(128)} %reg_weight.1, s32[4,32]{1,0:T(4,128)} %bricks.1, f32[4,8,512]{2,1,0:T(8,128)} %observed_hbm.1, f32[4,512]{1,0:T(4,128)} %data_weight_hbm.1, ...), custom_call_target="tpu_custom_call" | custom-call | tf_op jit(solution)/shard_map/inversion/pallas_call | solution.py:640
  97.4 1.4 %finish.1 = (f32[512,8,128]{2,1,0:T(8,128)}, f32[4,8,512]{2,1,0:T(8,128)}) custom-call(f32[512,8,128]{2,1,0:T(8,128)S(1)} %get-tuple-element.8.moved, f32[512,8,128]{2,1,0:T(8,128)S(1)} %get-tuple-element.9.gradient, f32[8,128]{1,0:T(8,128)S(1)} %get-tuple-element.10.step, f32[4,8,512]{2,1,0:T(8,128)S(1)} %get-tuple-element.11.misfit), custom_call_target="tpu_custom_call" | custom-call | tf_op jit(solution)/shard_map/finish/pallas_call | solution.py:715
